TPU v7x, 32 devices: a whole 2x2x4 slice. The times are simulated.
32 devices in a mesh: tile: 16 (over z, x, core), rep: 2 (over y).
Axes of the slice: x: 2, y: 2, z: 4, core: 2. Of those that a mesh axis runs over, the one named last changes fastest.
Arguments:
- waves: bfloat16 [2, 8192, 128], P('rep', 'tile'), may hold values from -6 to 6
- dest_tile: int32 [2, 8192, 1], P('rep', 'tile'), may hold values from 0 to 15; in each aligned block of 512 rows (0 to 511, 512 to 1023, ..., all dimensions but the last counted through in order) at most 32 rows name the same one
- pixel_bin: int32 [2, 8192], P('rep', 'tile'), may hold values from 0 to 1023
- target: float32 [2, 128, 128], P('rep', 'tile'), may hold values from -6 to 6
- conv_one: bfloat16 [3, 3, 128, 128], replicated, may hold values from -0.1875 to 0.1875
- bias_one: float32 [128], replicated, may hold values from -0.5 to 0.5
- conv_two: bfloat16 [3, 3, 128], replicated, may hold values from -0.1875 to 0.1875
- bias_two: float32 [1], replicated, may hold values from -1 to 1
Outputs:
- prediction: float32 [2, 128, 128], P('rep', 'tile')
- update_one: float32 [3, 3, 128, 128], replicated
- update_bias: float32 [128], replicated
- update_two: float32 [3, 3, 128], replicated
Inputs may be any that keep to these rules, and one draw needn't show every extreme that they name: `dest_tile`: among the rows of one device, no strip is named more than 32 times, a bound that some block reaches.
All inputs are finite; a program needn't handle non-finite values.
Results may differ from a plain program's by a relative error of at most 0.0024.
The roundings to bfloat16 on the way count: a program that leaves them out, or rounds other values in their place, can miss the bound.
Values may be sent and summed in bfloat16 or wider, within the bound.
A program may use at most 64 MiB of HBM per device.

v0:
```python
import math

import jax
import jax.numpy as jnp
from jax import lax
from jax.sharding import PartitionSpec as P

CAP = 32


def extended(block, sides, width):
    for axis, dim in sides:
        count = lax.axis_size(axis)
        forward = [(i, i + 1) for i in range(count - 1)]
        backward = [(target, source) for source, target in forward]
        low = lax.ppermute(
            lax.slice_in_dim(block, block.shape[dim] - width, None, axis=dim), axis, forward
        )
        high = lax.ppermute(lax.slice_in_dim(block, 0, width, axis=dim), axis, backward)
        block = jnp.concatenate([low, block, high], axis=dim)
    return block


def normalized(grad):
    return grad / jnp.sqrt(jnp.mean(grad * grad) + 1e-06)


def first_conv(padded, conv_one, bias_one, tall, width):
    steps = padded.shape[2]
    channels = conv_one.shape[3]
    pre = jnp.zeros((tall * width, channels), jnp.float32) + bias_one[None, :]
    for i in range(3):
        for j in range(3):
            patch = padded[2 * i : 2 * i + tall, 2 * j : 2 * j + width, :].reshape(
                tall * width, steps
            )
            pre = pre + jnp.dot(patch, conv_one[i, j], preferred_element_type=jnp.float32)
    return pre.reshape(tall, width, channels)


def second_conv(hidden_pad, conv_two, bias_two, tall, width):
    pred = jnp.zeros((tall, width), jnp.float32) + bias_two[0]
    for i in range(3):
        for j in range(3):
            pred = pred + jnp.einsum(
                "hwc,c->hw",
                hidden_pad[i : i + tall, j : j + width, :],
                conv_two[i, j],
                preferred_element_type=jnp.float32,
            )
    return pred


def on_device(waves, dest_tile, pixel_bin, target, conv_one, bias_one, conv_two, bias_two):
    tiles = lax.axis_size("tile")
    replicas = lax.axis_size("rep")
    steps = waves.shape[2]
    height = target.shape[1]
    width = target.shape[2]
    pixels = height * width
    channels = conv_one.shape[3]
    bucket = CAP
    tile_ids = dest_tile[0, :, 0]
    hits = (tile_ids[:, None] == jnp.arange(tiles, dtype=jnp.int32)[None, :]).astype(jnp.int32)
    rank = jnp.sum(jnp.cumsum(hits, axis=0) * hits, axis=1) - 1
    slots = tile_ids * bucket + rank
    send_wave = jnp.zeros((tiles * bucket, steps), jnp.bfloat16).at[slots].set(waves[0])
    send_bin = jnp.full((tiles * bucket,), -1, jnp.int32).at[slots].set(pixel_bin[0])
    recv_wave, recv_bin = (
        lax.all_to_all(
            send_wave.reshape(tiles, bucket, steps), "tile", split_axis=0, concat_axis=0, tiled=True
        ),
        lax.all_to_all(
            send_bin.reshape(tiles, bucket), "tile", split_axis=0, concat_axis=0, tiled=True
        ),
    )
    recv_wave = recv_wave.reshape(tiles * bucket, steps)
    recv_bin = recv_bin.reshape(tiles * bucket)
    block = math.gcd(pixels, 128)

    def raster(start):
        wanted = start + jnp.arange(block, dtype=jnp.int32)
        onehot = (wanted[:, None] == recv_bin[None, :]).astype(jnp.bfloat16)
        return jnp.dot(onehot, recv_wave, preferred_element_type=jnp.float32).astype(jnp.bfloat16)

    starts = jnp.arange(0, pixels, block, dtype=jnp.int32)
    grid = lax.map(raster, starts)
    padded = extended(grid, (("tile", 0),), 2)
    padded = jnp.pad(padded, ((0, 0), (2, 2), (0, 0)))
    pre = first_conv(padded, conv_one, bias_one, height, width)
    hidden = jax.nn.silu(pre).astype(jnp.bfloat16)
    hidden_pad = extended(hidden, (("tile", 0),), 1)
    hidden_pad = jnp.pad(hidden_pad, ((0, 0), (1, 1), (0, 0)))
    pred = second_conv(hidden_pad, conv_two, bias_two, height, width)
    error = ((pred - target[0]) / replicas).astype(jnp.bfloat16)
    error_pad = extended(error, (("tile", 0),), 1)
    error_pad = jnp.pad(error_pad, ((0, 0), (1, 1)))
    grad_two = []
    back = jnp.zeros((height, width, channels), jnp.float32)
    for i in range(3):
        for j in range(3):
            grad_two.append(
                jnp.einsum(
                    "hwc,hw->c",
                    hidden_pad[i : i + height, j : j + width, :],
                    error,
                    preferred_element_type=jnp.float32,
                )
            )
            shifted = error_pad[2 - i : 2 - i + height, 2 - j : 2 - j + width].astype(jnp.float32)
            back = back + shifted[:, :, None] * conv_two[i, j].astype(jnp.float32)[None, None, :]
    grad_two = jnp.stack(grad_two).reshape(3, 3, channels)
    sig = jax.nn.sigmoid(pre)
    slope = (back * sig * (1.0 + pre * (1.0 - sig))).astype(jnp.bfloat16)
    slope_flat = slope.reshape(pixels, channels)
    grad_one = []
    for i in range(3):
        for j in range(3):
            patch = padded[2 * i : 2 * i + height, 2 * j : 2 * j + width, :].reshape(pixels, steps)
            grad_one.append(
                lax.dot_general(
                    patch, slope_flat, (((0,), (0,)), ((), ())), preferred_element_type=jnp.float32
                )
            )
    grad_one = jnp.stack(grad_one).reshape(3, 3, steps, channels)
    grad_bias = jnp.sum(slope_flat.astype(jnp.float32), axis=0)
    share = lax.psum_scatter(
        grad_one.reshape(9 * steps, channels), "tile", scatter_dimension=0, tiled=True
    )
    share = lax.psum(share, "rep")
    grad_one = lax.all_gather(share, "tile", axis=0, tiled=True).reshape(3, 3, steps, channels)
    grad_bias, grad_two = lax.psum((grad_bias, grad_two), ("tile", "rep"))
    return (pred[None], normalized(grad_one), normalized(grad_bias), normalized(grad_two))


def solution(mesh):
    placed = (
        P("rep", "tile", None),
        P("rep", "tile", None),
        P("rep", "tile"),
        P("rep", "tile", None),
        P(),
        P(),
        P(),
        P(),
    )
    return jax.shard_map(
        on_device,
        mesh=mesh,
        in_specs=placed,
        out_specs=(P("rep", "tile", None), P(), P(), P()),
        check_vma=False,
    )
```

profile of v0, /device:TPU:1, one launch (start us, length us, event | category | flops | bytes accessed | tf_op | source)
XLA Modules:
  0.0 185.9 jit_solution(650408584183058171)
XLA Ops:
  7.2 0.7 fusion.75
  7.9 1.1 reduce-window.6
  9.3 0.8 fusion.56
  10.1 0.7 compare_select_fusion
  10.8 2.6 %scatter_custom_fusion = s32[512]{0:T(512)S(1)} fusion(s32[512]{0:T(512)S(1)} %bitcast.330, s32[512]{0:T(512)} %bitcast.332, s32[]{:T(128)} %constant.22.clone.1), kind=kCustom, calls=%fused_computation.156 | custom fusion | bytes 2560 | tf_op jit(solution)/shard_map/scatter | solution.py:68
  13.4 0.7 all_to_all.11
  14.1 7.3 %all-to-all-start = ((s32[16,1,32]{2,1,0:T(1,128)}), s32[16,1,32]{2,1,0:T(1,128)S(1)}, u32[]{:S(2)}, u32[]{:S(2)}) async-start(s32[16,1,32]{2,1,0:T(1,128)} %all_to_all.11), calls=%async_computation | async-start | bytes 16384 | tf_op jit(solution)/shard_map/all_to_all | solution.py:73
  21.4 2.4 %scatter_custom_fusion.1 = bf16[512,128]{1,0:T(8,128)(2,1)} fusion(s32[512]{0:T(512)S(1)} %bitcast.331, bf16[1,512,128]{2,1,0:T(8,128)(2,1)S(1)} %copy-done, bf16[]{:T(256)} %constant.14.clone.1), kind=kCustom, calls=%fused_computation.100 | custom fusion | bytes 262146 | tf_op jit(solution)/shard_map/scatter | solution.py:67
  23.7 3.4 %all-to-all-done = s32[16,1,32]{2,1,0:T(1,128)S(1)} async-done(((s32[16,1,32]{2,1,0:T(1,128)}), s32[16,1,32]{2,1,0:T(1,128)S(1)}, u32[]{:S(2)}, u32[]{:S(2)}) %all-to-all-start) | async-done | bytes 2080 | tf_op jit(solution)/shard_map/all_to_all | solution.py:73
  27.2 4.0 %all-to-all-start.1 = ((bf16[16,32,128]{2,1,0:T(8,128)(2,1)}), bf16[16,32,128]{2,1,0:T(8,128)(2,1)S(1)}, u32[]{:S(2)}, u32[]{:S(2)}) async-start(bf16[16,32,128]{2,1,0:T(8,128)(2,1)} %bitcast.12), calls=%async_computation.1 | async-start | bytes 262144 | tf_op jit(solution)/shard_map/all_to_all | solution.py:70
  31.3 6.8 %all-to-all-done.1 = bf16[16,32,128]{2,1,0:T(8,128)(2,1)S(1)} async-done(((bf16[16,32,128]{2,1,0:T(8,128)(2,1)}), bf16[16,32,128]{2,1,0:T(8,128)(2,1)S(1)}, u32[]{:S(2)}, u32[]{:S(2)}) %all-to-all-start.1) | async-done | bytes 131104 | tf_op jit(solution)/shard_map/all_to_all | solution.py:70
  38.1 12.0 %while.11 = (s32[]{:T(128)}, bf16[8,128,128]{2,1,0:T(8,128)(2,1)S(1)}, s32[8]{0:T(128)S(1)}, s32[16,32]{1,0:T(8,128)}, bf16[512,128]{1,0:T(8,128)(2,1)S(1)}, /*index=5*/s32[512]{0:T(512)S(1)}, s32[]{:T(128)}) while((s32[]{:T(128)}, bf16[8,128,128]{2,1,0:T(8,128)(2,1)S(1)}, s32[8]{0:T(128)S(1)}, s32[16,32]{1,0:T(8,128)}, ...), condition=%wide.wide.region_6.7_spmd, body=%wide.wide.region_5.6_spmd.sunk | while | flops 16859264 | bytes 167009 | solution.py:87
  38.1 0.6 dynamic_slice.6
  38.7 0.6 iota_add_fusion.3
  39.7 0.6 dynamic_slice.6
  40.2 0.6 iota_add_fusion.3
  41.2 0.6 dynamic_slice.6
  41.7 0.6 iota_add_fusion.3
  42.7 0.6 dynamic_slice.6
  43.3 0.6 iota_add_fusion.3
  44.2 0.6 dynamic_slice.6
  44.8 0.6 iota_add_fusion.3
  45.7 0.6 dynamic_slice.6
  46.3 0.6 iota_add_fusion.3
  47.2 0.6 dynamic_slice.6
  47.8 0.6 iota_add_fusion.3
  48.7 0.6 dynamic_slice.6
  49.3 0.6 iota_add_fusion.3
  50.4 2.1 %collective-permute-start = (bf16[2,128,128]{1,2,0:T(8,128)(2,1)S(1)}, bf16[2,128,128]{1,2,0:T(8,128)(2,1)S(1)}, u32[]{:S(2)}, u32[]{:S(2)}) collective-permute-start(bf16[2,128,128]{1,2,0:T(8,128)(2,1)S(1)} %get-tuple-element.57), channel_id=1, source_target_pairs={{0,2},{2,4},{4,6},{6,8},{8,10},{10,12},{12,14},{14,16},{16,18},{18... | collective-permute-start | bytes 196616 | tf_op jit(solution)/shard_map/ppermute | solution.py:16
  52.5 2.3 %collective-permute-start.1 = (bf16[2,128,128]{1,2,0:T(8,128)(2,1)S(1)}, bf16[2,128,128]{1,2,0:T(8,128)(2,1)S(1)}, u32[]{:S(2)}, u32[]{:S(2)}) collective-permute-start(bf16[2,128,128]{1,2,0:T(8,128)(2,1)S(1)} %get-tuple-element.58), channel_id=1, source_target_pairs={{2,0},{4,2},{6,4},{8,6},{10,8},{12,10},{14,12},{16,14},{18,16},{20... | collective-permute-start | bytes 196616 | tf_op jit(solution)/shard_map/ppermute | solution.py:19
  54.8 0.6 bitcast_convert_fusion.8
  56.1 2.0 %collective-permute-done.1 = bf16[2,128,128]{1,2,0:T(8,128)(2,1)S(1)} collective-permute-done((bf16[2,128,128]{1,2,0:T(8,128)(2,1)S(1)}, bf16[2,128,128]{1,2,0:T(8,128)(2,1)S(1)}, u32[]{:S(2)}, u32[]{:S(2)}) %collective-permute-start.1) | collective-permute-done | bytes 65568 | tf_op jit(solution)/shard_map/ppermute | solution.py:19
  58.1 0.6 copy-done.4
  58.7 0.4 fusion.19
  59.1 0.4 fusion.137
  59.7 0.9 pad_maximum_fusion.2
  60.6 0.9 copy.39
  61.4 0.8 copy.40
  63.2 1.0 convolution_add_fusion.8
  64.5 0.7 copy-done.1
  66.5 0.3 multiply_convert_fusion.2
  67.0 1.9 %collective-permute-start.2 = (bf16[1,128,128]{2,1,0:T(8,128)(2,1)S(1)}, bf16[1,128,128]{2,1,0:T(8,128)(2,1)S(1)}, u32[]{:S(2)}, u32[]{:S(2)}) collective-permute-start(bf16[1,128,128]{2,1,0:T(8,128)(2,1)S(1)} %get-tuple-element.53), channel_id=1, source_target_pairs={{0,2},{2,4},{4,6},{6,8},{8,10},{10,12},{12,14},{14,16},{16,18},{18... | collective-permute-start | bytes 98312 | tf_op jit(solution)/shard_map/ppermute | solution.py:16
  68.9 2.4 %collective-permute-start.3 = (bf16[1,128,128]{2,1,0:T(8,128)(2,1)S(1)}, bf16[1,128,128]{2,1,0:T(8,128)(2,1)S(1)}, u32[]{:S(2)}, u32[]{:S(2)}) collective-permute-start(bf16[1,128,128]{2,1,0:T(8,128)(2,1)S(1)} %get-tuple-element.54), channel_id=1, source_target_pairs={{2,0},{4,2},{6,4},{8,6},{10,8},{12,10},{14,12},{16,14},{18,16},{20... | collective-permute-start | bytes 98312 | tf_op jit(solution)/shard_map/ppermute | solution.py:19
  71.5 3.4 %collective-permute-done.3 = bf16[1,128,128]{2,1,0:T(8,128)(2,1)S(1)} collective-permute-done((bf16[1,128,128]{2,1,0:T(8,128)(2,1)S(1)}, bf16[1,128,128]{2,1,0:T(8,128)(2,1)S(1)}, u32[]{:S(2)}, u32[]{:S(2)}) %collective-permute-start.3) | collective-permute-done | bytes 32800 | tf_op jit(solution)/shard_map/ppermute | solution.py:19
  76.6 0.6 convert_bitcast_fusion
  78.4 1.9 %collective-permute-start.4 = (bf16[1,128]{1,0:T(2,128)(2,1)S(1)}, bf16[1,128]{1,0:T(2,128)(2,1)S(1)}, u32[]{:S(2)}, u32[]{:S(2)}) collective-permute-start(bf16[1,128]{1,0:T(2,128)(2,1)S(1)} %get-tuple-element.87), channel_id=1, source_target_pairs={{0,2},{2,4},{4,6},{6,8},{8,10},{10,12},{12,14},{14,16},{16,18},{18... | collective-permute-start | bytes 776 | tf_op jit(solution)/shard_map/ppermute | solution.py:16
  80.3 2.4 %collective-permute-start.5 = (bf16[1,128]{1,0:T(2,128)(2,1)S(1)}, bf16[1,128]{1,0:T(2,128)(2,1)S(1)}, u32[]{:S(2)}, u32[]{:S(2)}) collective-permute-start(bf16[1,128]{1,0:T(2,128)(2,1)S(1)} %get-tuple-element.88), channel_id=1, source_target_pairs={{2,0},{4,2},{6,4},{8,6},{10,8},{12,10},{14,12},{16,14},{18,16},{20... | collective-permute-start | bytes 776 | tf_op jit(solution)/shard_map/ppermute | solution.py:19
  83.1 3.0 %collective-permute-done.5 = bf16[1,128]{1,0:T(2,128)(2,1)S(1)} collective-permute-done((bf16[1,128]{1,0:T(2,128)(2,1)S(1)}, bf16[1,128]{1,0:T(2,128)(2,1)S(1)}, u32[]{:S(2)}, u32[]{:S(2)}) %collective-permute-start.5) | collective-permute-done | bytes 288 | tf_op jit(solution)/shard_map/ppermute | solution.py:19
  86.3 1.6 multiply_convert_fusion.1
  88.4 0.3 fusion.13
  89.2 0.3 fusion.10
  90.0 0.3 fusion.8
  90.3 0.8 copy-done.3
  91.1 1.6 convert_reduce_fusion
  92.8 39.3 %all-reduce.4 = (f32[128]{0:T(128)S(1)}, f32[3,3,128]{2,1,0:T(4,128)S(1)}) all-reduce(f32[128]{0:T(128)S(1)} %convert_reduce_fusion, f32[3,3,128]{2,1,0:T(4,128)S(1)} %reshape.152), channel_id=1, replica_groups=mesh['tile'=16,'rep'=2] {'tile','rep'}, use_global_device_ids=true, to_apply=%region_11.12 | all-reduce | flops 1280 | bytes 10240 | tf_op jit(solution)/shard_map/psum | solution.py:132
  132.0 0.6 multiply_reduce_fusion.1
  133.3 0.6 multiply_reduce_fusion.2
  134.6 0.5 broadcast_divide_fusion.2
  135.2 0.6 broadcast_divide_fusion.1
  135.8 8.4 %reduce-scatter.4.cloned.1.call-done = f32[72,128]{1,0:T(8,128)} async-done(((f32[1152,128]{1,0:T(8,128)}), f32[72,128]{1,0:T(8,128)}) %reduce-scatter.4.cloned.1.call-update) | async-done | bytes 36880
  144.2 7.0 %psum.21 = f32[72,128]{1,0:T(8,128)S(1)} all-reduce(f32[72,128]{1,0:T(8,128)} %reduce-scatter.4.cloned.1.call-done), channel_id=1, replica_groups=mesh['tile'=16,'rep'=2] {'rep'}, use_global_device_ids=true, to_apply=%region_8.9 | all-reduce | flops 9216 | bytes 73728 | tf_op jit(solution)/shard_map/psum | solution.py:130
  151.2 25.5 %all_gather.3 = f32[1152,128]{1,0:T(8,128)S(1)} all-gather(f32[72,128]{1,0:T(8,128)S(1)} %psum.21), channel_id=1, replica_groups=mesh['tile'=16,'rep'=2] {'tile'}, dimensions={0}, use_global_device_ids=true | all-gather | bytes 626688 | tf_op jit(solution)/shard_map/all_gather | solution.py:131
  176.8 0.7 multiply_reduce_fusion
  178.2 0.9 broadcast_divide_fusion
  (101 shorter events, 10.3 us)
Async XLA Ops:
  7.2 14.2 %copy-start = (bf16[1,512,128]{2,1,0:T(8,128)(2,1)S(1)}, bf16[1,512,128]{2,1,0:T(8,128)(2,1)}, u32[]{:S(2)}) copy-start(bf16[1,512,128]{2,1,0:T(8,128)(2,1)} %param.10) | copy-start | bytes 393220
  14.1 13.1 %all-to-all-start = ((s32[16,1,32]{2,1,0:T(1,128)}), s32[16,1,32]{2,1,0:T(1,128)S(1)}, u32[]{:S(2)}, u32[]{:S(2)}) async-start(s32[16,1,32]{2,1,0:T(1,128)} %all_to_all.11), calls=%async_computation | async-start | bytes 16384 | tf_op jit(solution)/shard_map/all_to_all | solution.py:73
  27.2 11.0 %copy-start.9 = (s32[16,1,32]{2,1,0:T(1,128)}, s32[16,1,32]{2,1,0:T(1,128)S(1)}, u32[]{:S(2)}) copy-start(s32[16,1,32]{2,1,0:T(1,128)S(1)} %all-to-all-done) | copy-start | bytes 6148
  27.2 11.0 %all-to-all-start.1 = ((bf16[16,32,128]{2,1,0:T(8,128)(2,1)}), bf16[16,32,128]{2,1,0:T(8,128)(2,1)S(1)}, u32[]{:S(2)}, u32[]{:S(2)}) async-start(bf16[16,32,128]{2,1,0:T(8,128)(2,1)} %bitcast.12), calls=%async_computation.1 | async-start | bytes 262144 | tf_op jit(solution)/shard_map/all_to_all | solution.py:70
  31.2 113.0 %reduce-scatter.4.cloned.1.call-start = ((), (), s32[]{:S(2)}) async-start(), calls=%async_computation.3 | async-start | bytes 626688
  38.1 16.6 %copy-start.10 = (bf16[3,3,128]{2,1,0:T(4,128)(2,1)S(1)}, bf16[3,3,128]{2,1,0:T(4,128)(2,1)}, u32[]{:S(2)}) copy-start(bf16[3,3,128]{2,1,0:T(4,128)(2,1)} %param.16) | copy-start | bytes 6916
  50.4 5.7 %collective-permute-start = (bf16[2,128,128]{1,2,0:T(8,128)(2,1)S(1)}, bf16[2,128,128]{1,2,0:T(8,128)(2,1)S(1)}, u32[]{:S(2)}, u32[]{:S(2)}) collective-permute-start(bf16[2,128,128]{1,2,0:T(8,128)(2,1)S(1)} %get-tuple-element.57), channel_id=1, source_target_pairs={{0,2},{2,4},{4,6},{6,8},{8,10},{10,12},{12,14},{14,16},{16,18},{18... | collective-permute-start | bytes 196616 | tf_op jit(solution)/shard_map/ppermute | solution.py:16
  52.5 5.6 %collective-permute-start.1 = (bf16[2,128,128]{1,2,0:T(8,128)(2,1)S(1)}, bf16[2,128,128]{1,2,0:T(8,128)(2,1)S(1)}, u32[]{:S(2)}, u32[]{:S(2)}) collective-permute-start(bf16[2,128,128]{1,2,0:T(8,128)(2,1)S(1)} %get-tuple-element.58), channel_id=1, source_target_pairs={{2,0},{4,2},{6,4},{8,6},{10,8},{12,10},{14,12},{16,14},{18,16},{20... | collective-permute-start | bytes 196616 | tf_op jit(solution)/shard_map/ppermute | solution.py:19
  56.1 2.0 %copy-start.6 = (bf16[2,128,128]{1,2,0:T(8,128)(2,1)}, bf16[2,128,128]{1,2,0:T(8,128)(2,1)S(1)}, u32[]{:S(2)}) copy-start(bf16[2,128,128]{1,2,0:T(8,128)(2,1)S(1)} %collective-permute-done) | copy-start | bytes 196612
  58.1 0.6 copy-start.4
  63.0 1.3 copy-start.2
  63.2 1.1 copy-start.8
  64.3 1.0 copy-start.1
  67.0 4.5 %collective-permute-start.2 = (bf16[1,128,128]{2,1,0:T(8,128)(2,1)S(1)}, bf16[1,128,128]{2,1,0:T(8,128)(2,1)S(1)}, u32[]{:S(2)}, u32[]{:S(2)}) collective-permute-start(bf16[1,128,128]{2,1,0:T(8,128)(2,1)S(1)} %get-tuple-element.53), channel_id=1, source_target_pairs={{0,2},{2,4},{4,6},{6,8},{8,10},{10,12},{12,14},{14,16},{16,18},{18... | collective-permute-start | bytes 98312 | tf_op jit(solution)/shard_map/ppermute | solution.py:16
  68.9 6.0 %collective-permute-start.3 = (bf16[1,128,128]{2,1,0:T(8,128)(2,1)S(1)}, bf16[1,128,128]{2,1,0:T(8,128)(2,1)S(1)}, u32[]{:S(2)}, u32[]{:S(2)}) collective-permute-start(bf16[1,128,128]{2,1,0:T(8,128)(2,1)S(1)} %get-tuple-element.54), channel_id=1, source_target_pairs={{2,0},{4,2},{6,4},{8,6},{10,8},{12,10},{14,12},{16,14},{18,16},{20... | collective-permute-start | bytes 98312 | tf_op jit(solution)/shard_map/ppermute | solution.py:19
  75.9 0.7 copy-start.17
  78.2 8.1 %copy-start.11 = (f32[128]{0:T(128)S(1)}, f32[128]{0:T(128)}, u32[]{:S(2)}) copy-start(f32[128]{0:T(128)} %get-tuple-element.74) | copy-start | bytes 1540
  78.2 8.1 %copy-start.12 = (f32[128]{0:T(128)S(1)}, f32[128]{0:T(128)}, u32[]{:S(2)}) copy-start(f32[128]{0:T(128)} %get-tuple-element.75) | copy-start | bytes 1540
  78.2 8.1 %copy-start.13 = (f32[128]{0:T(128)S(1)}, f32[128]{0:T(128)}, u32[]{:S(2)}) copy-start(f32[128]{0:T(128)} %get-tuple-element.76) | copy-start | bytes 1540
  78.2 8.1 %copy-start.14 = (f32[128]{0:T(128)S(1)}, f32[128]{0:T(128)}, u32[]{:S(2)}) copy-start(f32[128]{0:T(128)} %get-tuple-element.77) | copy-start | bytes 1540
  78.2 8.1 %copy-start.15 = (f32[128]{0:T(128)S(1)}, f32[128]{0:T(128)}, u32[]{:S(2)}) copy-start(f32[128]{0:T(128)} %get-tuple-element.78) | copy-start | bytes 1540
  78.2 8.1 %copy-start.16 = (f32[128]{0:T(128)S(1)}, f32[128]{0:T(128)}, u32[]{:S(2)}) copy-start(f32[128]{0:T(128)} %get-tuple-element.79) | copy-start | bytes 1540
  78.4 4.7 %collective-permute-start.4 = (bf16[1,128]{1,0:T(2,128)(2,1)S(1)}, bf16[1,128]{1,0:T(2,128)(2,1)S(1)}, u32[]{:S(2)}, u32[]{:S(2)}) collective-permute-start(bf16[1,128]{1,0:T(2,128)(2,1)S(1)} %get-tuple-element.87), channel_id=1, source_target_pairs={{0,2},{2,4},{4,6},{6,8},{8,10},{10,12},{12,14},{14,16},{16,18},{18... | collective-permute-start | bytes 776 | tf_op jit(solution)/shard_map/ppermute | solution.py:16
  80.3 5.8 %collective-permute-start.5 = (bf16[1,128]{1,0:T(2,128)(2,1)S(1)}, bf16[1,128]{1,0:T(2,128)(2,1)S(1)}, u32[]{:S(2)}, u32[]{:S(2)}) collective-permute-start(bf16[1,128]{1,0:T(2,128)(2,1)S(1)} %get-tuple-element.88), channel_id=1, source_target_pairs={{2,0},{4,2},{6,4},{8,6},{10,8},{12,10},{14,12},{16,14},{18,16},{20... | collective-permute-start | bytes 776 | tf_op jit(solution)/shard_map/ppermute | solution.py:19
  83.0 5.1 %copy-start.7 = (bf16[2,128,128]{1,2,0:T(8,128)(2,1)S(1)}, bf16[2,128,128]{1,2,0:T(8,128)(2,1)}, u32[]{:S(2)}) copy-start(bf16[2,128,128]{1,2,0:T(8,128)(2,1)} %copy-done.6) | copy-start | bytes 196612
  88.9 0.8 copy-start.5
  90.3 0.8 copy-start.3
Sparse Core Ops, SparseCore 0:
  91.3 52.8 reduce-scatter.3
where the time goes:
time: 187 us; the launch traced here: 186 us
  blocking collectives  71.8 us (38%)
  waiting for transfers between devices  27 us (14%)
  starting transfers between devices  24.4 us (13%)
  other arithmetic  18.6 us (10%)
  between operations  17.3 us (9%)
  local copies, waits for them, and re-layouts  16.4 us (9%)
  matrix products  10.1 us (5%)
    psum x1, blocking collectives, on_device(): grad_bias, grad_two = lax.psum((grad_bias, grad_two), ('tile', 'rep'))  39.3 us
    all_gather x1, blocking collectives, on_device(): lax.all_gather(share, 'tile', axis=0, tiled=True)  25.5 us
    unnamed x2, waiting for transfers between devices  8.45 us
    ppermute x3, waiting for transfers between devices, extended(): lax.ppermute(lax.slice_in_dim(block, 0, width, axis=dim), axis, backward)  8.33 us
    all_to_all x1, starting transfers between devices, on_device(): lax.all_to_all(send_bin.reshape(tiles, bucket), 'tile', split_axis=0, con...  7.32 us
    ppermute x3, starting transfers between devices, extended(): lax.ppermute(lax.slice_in_dim(block, 0, width, axis=dim), axis, backward)  7.12 us
    psum x1, blocking collectives, on_device(): share = lax.psum(share, 'rep')  7.05 us
    all_to_all x1, waiting for transfers between devices, on_device(): lax.all_to_all(send_wave.reshape(tiles, bucket, steps), 'tile', split_axi...  6.81 us
  transfers between devices with their start and end apart: 9, of which 6 were waited for; matrix products, arithmetic and copies ran while one was open for 4% of the time, Pallas kernels for 0%

commit v1 on v0

v1 whole, which is shorter than its diff:
```python
import functools

import jax
import jax.numpy as jnp
from jax import lax
from jax.experimental import pallas as pl
from jax.experimental.pallas import tpu as pltpu
from jax.sharding import PartitionSpec as P

CAP = 32
HALO = 4
MESH = pl.DeviceIdType.MESH
F32 = jnp.float32
BF16 = jnp.bfloat16


def iota(shape, dim):
    return lax.broadcasted_iota(jnp.int32, shape, dim)


def dot(a, b, dims=((1,), (0,))):
    return lax.dot_general(a, b, (dims, ((), ())), preferred_element_type=F32)


def step_kernel(
    tiles, reps, part,
    dest_ref, bin_ref, waves_ref, target_ref, w1_ref, b1_ref, w2_ref, b2_ref,
    pred_ref, u1_ref, ub_ref, u2_ref,
    sendw, sendb, recvw, recvb, grid, wide, pre_s, hid_s, tlow, thigh, w2_s, taps, etap,
    full, pair, total, recvs, gathered, flat,
    aw_send, aw_recv, ab_send, ab_recv, t_send, t_recv, g_send, g_recv,
    p_send, p_recv, r_send, r_recv, n_send, n_recv, f_send, f_recv,
):
    me = lax.axis_index("tile")
    rep = lax.axis_index("rep")
    rows, steps = waves_ref.shape
    height, width = target_ref.shape
    channels = b1_ref.shape[1]
    half = tiles // 2
    groups = half * reps
    core = lax.rem(me, 2)
    partner = me + 1 - 2 * core
    chip = rep * half + me // 2
    pixels = height * width
    tall = height + HALO

    def tile_peer(k):
        return lax.rem(me + k, tiles)

    def group_peer(k):
        q = lax.rem(chip + k, groups)
        return q, {"tile": 2 * lax.rem(q, half) + core, "rep": q // half}

    barrier = pltpu.get_barrier_semaphore()

    def greet(k, carry):
        pl.semaphore_signal(barrier, inc=1, device_id={"tile": tile_peer(k), "rep": rep}, device_id_type=MESH)
        return carry

    lax.fori_loop(1, tiles, greet, 0)

    def greet_far(k, carry):
        pl.semaphore_signal(
            barrier,
            inc=1,
            device_id={"tile": 2 * lax.rem(k, half) + core, "rep": lax.rem(rep + 1 + k // half, reps)},
            device_id_type=MESH,
        )
        return carry

    lax.fori_loop(0, (reps - 1) * half, greet_far, 0)

    hits = (iota((tiles, rows), 0) == dest_ref[...]).astype(F32)
    earlier = (iota((rows, rows), 0) < iota((rows, rows), 1)).astype(F32).astype(BF16)
    ranks = dot(hits.astype(BF16), earlier)
    rank = jnp.sum(hits * ranks, axis=0, keepdims=True)
    slot = jnp.sum(hits * (ranks + (CAP * iota((tiles, rows), 0)).astype(F32)), axis=0, keepdims=True)
    place = (iota((tiles * CAP, rows), 0).astype(F32) == slot).astype(F32).astype(BF16)
    sendw[...] = dot(place, waves_ref[...]).astype(BF16)
    lane = rank + (CAP * lax.rem(me, 4)).astype(F32)
    lanes = (iota((128, rows), 0).astype(F32) == lane).astype(F32).astype(BF16)
    bins = bin_ref[...]
    high = (bins // 32).astype(F32)
    low = (bins - 32 * (bins // 32)).astype(F32)
    named = 32.0 * dot((hits * high).astype(BF16), lanes, ((1,), (1,))) + dot(
        (hits * low).astype(BF16), lanes, ((1,), (1,))
    )
    for t in range(tiles):
        sendb[t] = named[t : t + 1, :]

    pl.semaphore_wait(barrier, tiles - 1 + (reps - 1) * half)

    def wave_copy(peer, source):
        return pltpu.make_async_remote_copy(
            src_ref=sendw.at[pl.ds(pl.multiple_of(peer * CAP, CAP), CAP)],
            dst_ref=recvw.at[pl.ds(pl.multiple_of(source * CAP, CAP), CAP)],
            send_sem=aw_send.at[peer],
            recv_sem=aw_recv.at[source],
            device_id={"tile": peer, "rep": rep},
            device_id_type=MESH,
        )

    def bin_copy(peer, source):
        return pltpu.make_async_remote_copy(
            src_ref=sendb.at[peer],
            dst_ref=recvb.at[source],
            send_sem=ab_send.at[peer],
            recv_sem=ab_recv.at[source],
            device_id={"tile": peer, "rep": rep},
            device_id_type=MESH,
        )

    def scatter(k, carry):
        peer = tile_peer(k)
        wave_copy(peer, me).start()
        bin_copy(peer, me).start()
        return carry

    lax.fori_loop(1, tiles, scatter, 0)

    up = jnp.minimum(me + 1, tiles - 1)
    down = jnp.maximum(me - 1, 0)
    span = HALO * width

    def target_copy(peer, dst, k):
        return pltpu.make_async_remote_copy(
            src_ref=target_ref, dst_ref=dst, send_sem=t_send.at[k], recv_sem=t_recv.at[k],
            device_id={"tile": peer, "rep": rep}, device_id_type=MESH,
        )

    def halo_copy(peer, src, dst, k):
        return pltpu.make_async_remote_copy(
            src_ref=grid.at[pl.ds(src, span)], dst_ref=grid.at[pl.ds(dst, span)],
            send_sem=g_send.at[k], recv_sem=g_recv.at[k],
            device_id={"tile": peer, "rep": rep}, device_id_type=MESH,
        )

    to_up = target_copy(up, tlow, 0)
    to_down = target_copy(down, thigh, 1)
    grid_up = halo_copy(up, span + pixels - span, 0, 0)
    grid_down = halo_copy(down, span, span + pixels, 1)
    has_up = me < tiles - 1
    has_down = me > 0

    @pl.when(has_up)
    def _():
        to_up.start()

    @pl.when(has_down)
    def _():
        to_down.start()

    @pl.when(jnp.logical_not(has_down))
    def _():
        grid[0:span, :] = jnp.zeros((span, steps), BF16)
        tlow[...] = jnp.zeros((height, width), F32)

    @pl.when(jnp.logical_not(has_up))
    def _():
        grid[span + pixels : span + pixels + span, :] = jnp.zeros((span, steps), BF16)
        thigh[...] = jnp.zeros((height, width), F32)

    own = pl.ds(pl.multiple_of(me * CAP, CAP), CAP)
    recvw[own, :] = sendw[own, :]
    recvb[me] = sendb[me]
    w2_s[...] = jnp.zeros(w2_s.shape, F32)
    for i in range(3):
        w2_s[8 * i : 8 * i + 3, :] = w2_ref[i].astype(F32)
    w2 = w2_s[...].astype(BF16)

    def arrive(k, carry):
        peer = tile_peer(k)
        wave_copy(peer, peer).wait_recv()
        bin_copy(peer, peer).wait_recv()
        return carry

    lax.fori_loop(1, tiles, arrive, 0)

    names = []
    for q in range(tiles // 4):
        names.append(recvb[4 * q] + recvb[4 * q + 1] + recvb[4 * q + 2] + recvb[4 * q + 3])
    names = jnp.concatenate(names, axis=1)
    block = 256
    order = [0, pixels - block] + [s for s in range(block, pixels - block, block)]
    for start in order:
        wanted = (iota((block, tiles * CAP), 0) + start).astype(F32)
        onehot = (wanted == names).astype(F32).astype(BF16)
        grid[span + start : span + start + block, :] = dot(onehot, recvw[...]).astype(BF16)

    @pl.when(has_up)
    def _():
        grid_up.start()

    @pl.when(has_down)
    def _():
        grid_down.start()

    column = iota((width, steps), 0)

    def spread(y):
        line = grid[y * width : (y + 1) * width, :]
        value = line.astype(F32)
        left = jnp.where(column >= 2, pltpu.roll(value, 2, 0), 0.0)
        right = jnp.where(column < width - 2, pltpu.roll(value, width - 2, 0), 0.0)
        wide[y * width : (y + 1) * width, 0:steps] = left.astype(BF16)
        wide[y * width : (y + 1) * width, steps : 2 * steps] = line
        wide[y * width : (y + 1) * width, 2 * steps : 3 * steps] = right.astype(BF16)

    for y in range(HALO, HALO + height):
        spread(y)

    @pl.when(has_down)
    def _():
        grid_up.wait_recv()

    @pl.when(has_up)
    def _():
        grid_down.wait_recv()

    for y in list(range(HALO)) + list(range(HALO + height, 2 * HALO + height)):
        spread(y)

    bias = b1_ref[...]
    for y in range(0, tall, 2):
        acc = jnp.zeros((2 * width, channels), F32) + bias
        for i in range(3):
            acc = acc + dot(wide[(y + 2 * i) * width : (y + 2 * i + 2) * width, :], w1_ref[i])
        sig = 1.0 / (1.0 + jnp.exp(-acc))
        hidden = acc * sig
        if y < 2:
            hidden = jnp.where(has_down, hidden, 0.0)
        if y >= height + 2:
            hidden = jnp.where(has_up, hidden, 0.0)
        hid_s[y * width : (y + 2) * width, :] = hidden.astype(BF16)
        if 2 <= y < height + 2:
            pre_s[(y - 2) * width : y * width, :] = sig * (1.0 + acc * (1.0 - sig))

    each = dot(w2, hid_s[...], ((1,), (1,)))
    span2 = (height + 2) * width
    summed = each[0:8, 0:span2] + each[8:16, width : width + span2] + each[16:24, 2 * width : 2 * width + span2]
    taps[...] = jnp.zeros(taps.shape, F32)
    for y in range(height + 2):
        for j in range(3):
            taps[j, y : y + 1, :] = summed[j : j + 1, y * width : (y + 1) * width]
    tp = taps.shape[1]
    x_at = iota((tp, width), 1)
    y_at = iota((tp, width), 0)
    pred = (
        b2_ref[0]
        + jnp.where(x_at >= 1, pltpu.roll(taps[0], 1, 1), 0.0)
        + taps[1]
        + jnp.where(x_at < width - 1, pltpu.roll(taps[2], width - 1, 1), 0.0)
    )

    @pl.when(has_down)
    def _():
        to_up.wait_recv()

    @pl.when(has_up)
    def _():
        to_down.wait_recv()

    taps[3] = pred
    pred_ref[...] = taps[3, 1 : 1 + height, :]
    taps[4, 0:1, :] = tlow[height - 1 : height, :]
    taps[4, 1 : 1 + height, :] = target_ref[...]
    taps[4, 1 + height : 2 + height, :] = thigh[0:1, :]
    inside = jnp.logical_and(
        jnp.logical_or(y_at >= 1, has_down),
        jnp.logical_and(y_at < height + 2, jnp.logical_or(y_at < height + 1, has_up)),
    )
    error = jnp.where(inside, (pred - taps[4]) / reps, 0.0).astype(BF16).astype(F32)
    taps[0] = jnp.where(x_at < width - 1, pltpu.roll(error, width - 1, 1), 0.0)
    taps[1] = error
    taps[2] = jnp.where(x_at >= 1, pltpu.roll(error, 1, 1), 0.0)
    etap[...] = jnp.zeros(etap.shape, F32)
    for i in range(3):
        for j in range(3):
            for y in range(height):
                etap[8 * i + j : 8 * i + j + 1, y * width : (y + 1) * width] = taps[j, y + 2 - i : y + 3 - i, :]
    errors = etap[...].astype(BF16)

    mine = hid_s[2 * width : 2 * width + pixels, :]
    grad_two = dot(errors, mine)
    back = dot(errors, w2, ((0,), (0,)))
    slope = (back * pre_s[...]).astype(BF16)
    grad_bias = dot(jnp.ones((8, pixels), BF16), slope)
    piece = steps // 2
    small = 9 * piece
    for h in range(2):
        full[h, small : small + 24, :] = grad_two
        full[h, small + 24 : small + 32, :] = grad_bias
        if full.shape[1] > small + 32:
            full[h, small + 32 :, :] = jnp.zeros((full.shape[1] - small - 32, channels), F32)
    for i in range(3):
        start = (2 + 2 * i) * width
        g = dot(wide[start : start + pixels, :], slope, ((0,), (0,)))
        for j in range(3):
            k = 3 * i + j
            for h in range(2):
                full[h, k * piece : (k + 1) * piece, :] = g[j * steps + h * piece : j * steps + (h + 1) * piece, :]

    swap = pltpu.make_async_remote_copy(
        src_ref=full.at[1 - core], dst_ref=pair, send_sem=p_send, recv_sem=p_recv,
        device_id={"tile": partner, "rep": rep}, device_id_type=MESH,
    )
    swap.start()
    swap.wait_recv()
    total[...] = full[core] + pair[...]

    def share_copy(q, device, source):
        return pltpu.make_async_remote_copy(
            src_ref=total.at[pl.ds(pl.multiple_of(q * part, 8), part)], dst_ref=recvs.at[source],
            send_sem=r_send.at[q], recv_sem=r_recv.at[source], device_id=device, device_id_type=MESH,
        )

    def give(k, carry):
        q, device = group_peer(k)
        share_copy(q, device, chip).start()
        return carry

    lax.fori_loop(1, groups, give, 0)
    recvs[chip] = total[pl.ds(pl.multiple_of(chip * part, 8), part), :]

    def take(k, carry):
        q, device = group_peer(k)
        share_copy(q, device, q).wait_recv()
        return carry

    lax.fori_loop(1, groups, take, 0)
    share = lax.fori_loop(1, groups, lambda q, acc: acc + recvs[q], recvs[0])
    gathered[core, chip] = share.astype(BF16)

    def spread_copy(device, source):
        return pltpu.make_async_remote_copy(
            src_ref=gathered.at[core, chip], dst_ref=gathered.at[core, source],
            send_sem=n_send.at[source], recv_sem=n_recv.at[source], device_id=device, device_id_type=MESH,
        )

    def spread_start(k, carry):
        q, device = group_peer(k)
        pltpu.make_async_remote_copy(
            src_ref=gathered.at[core, chip], dst_ref=gathered.at[core, chip],
            send_sem=n_send.at[q], recv_sem=n_recv.at[chip], device_id=device, device_id_type=MESH,
        ).start()
        return carry

    lax.fori_loop(1, groups, spread_start, 0)

    def forward(q, which):
        return pltpu.make_async_remote_copy(
            src_ref=gathered.at[which, q], dst_ref=gathered.at[which, q],
            send_sem=f_send.at[q], recv_sem=f_recv.at[q],
            device_id={"tile": partner, "rep": rep}, device_id_type=MESH,
        )

    forward(chip, core).start()

    def pass_on(k, carry):
        q, device = group_peer(groups - k)
        spread_copy(device, q).wait_recv()
        forward(q, core).start()
        return carry

    lax.fori_loop(1, groups, pass_on, 0)

    def finish(q, carry):
        forward(q, 1 - core).wait_recv()
        return carry

    lax.fori_loop(0, groups, finish, 0)

    def normalized(g, count, sums):
        return g / jnp.sqrt(sums / count + 1e-06)

    for h in range(2):
        flat[h] = gathered[h].astype(F32).reshape(groups * part, channels)
    one = flat[:, 0:small, :]
    scale = jnp.sqrt(jnp.sum(one * one) / (9 * steps * channels) + 1e-06)
    for k in range(9):
        for h in range(2):
            u1_ref[k // 3, k % 3, h * piece : (h + 1) * piece, :] = flat[h, k * piece : (k + 1) * piece, :] / scale
    two = flat[0, small : small + 24, :]
    two = two / jnp.sqrt(jnp.sum(two * two) / (9 * channels) + 1e-06)
    for i in range(3):
        u2_ref[i] = two[8 * i : 8 * i + 3, :]
    gb = flat[0, small + 24 : small + 25, :]
    ub_ref[...] = gb / jnp.sqrt(jnp.sum(gb * gb) / channels + 1e-06)

    @pl.when(has_up)
    def _():
        to_up.wait_send()
        grid_up.wait_send()

    @pl.when(has_down)
    def _():
        to_down.wait_send()
        grid_down.wait_send()

    def sent(k, carry):
        peer = tile_peer(k)
        wave_copy(peer, me).wait_send()
        bin_copy(peer, me).wait_send()
        return carry

    lax.fori_loop(1, tiles, sent, 0)
    swap.wait_send()

    def shared(k, carry):
        q, device = group_peer(k)
        share_copy(q, device, chip).wait_send()
        spread_copy(device, q).wait_send()
        return carry

    lax.fori_loop(1, groups, shared, 0)

    def passed(q, carry):
        forward(q, core).wait_send()
        return carry

    lax.fori_loop(0, groups, passed, 0)


def on_device(tiles, reps, waves, dest_tile, pixel_bin, target, conv_one, bias_one, conv_two, bias_two):
    rows, steps = waves.shape[1:]
    height, width = target.shape[1:]
    channels = conv_one.shape[3]
    pixels = height * width
    groups = tiles // 2 * reps
    small = 9 * (steps // 2)
    part = -(-(small + 32) // (8 * groups)) * 8
    padded = groups * part
    tp = -(-(height + 2) // 8) * 8
    dma = pltpu.SemaphoreType.DMA
    vmem = pl.BlockSpec(memory_space=pltpu.VMEM)
    pred, one, bias, two = pl.pallas_call(
        functools.partial(step_kernel, tiles, reps, part),
        out_shape=(
            jax.ShapeDtypeStruct((height, width), F32),
            jax.ShapeDtypeStruct((3, 3, steps, channels), F32),
            jax.ShapeDtypeStruct((1, channels), F32),
            jax.ShapeDtypeStruct((3, 3, channels), F32),
        ),
        in_specs=[vmem] * 7 + [pl.BlockSpec(memory_space=pltpu.SMEM)],
        out_specs=(vmem,) * 4,
        scratch_shapes=[
            pltpu.VMEM((tiles * CAP, steps), BF16),
            pltpu.VMEM((tiles, 1, 128), F32),
            pltpu.VMEM((tiles * CAP, steps), BF16),
            pltpu.VMEM((tiles, 1, 128), F32),
            pltpu.VMEM(((height + 2 * HALO) * width, steps), BF16),
            pltpu.VMEM(((height + 2 * HALO) * width, 3 * steps), BF16),
            pltpu.VMEM((pixels, channels), F32),
            pltpu.VMEM(((height + HALO) * width, channels), BF16),
            pltpu.VMEM((height, width), F32),
            pltpu.VMEM((height, width), F32),
            pltpu.VMEM((24, channels), F32),
            pltpu.VMEM((5, tp, width), F32),
            pltpu.VMEM((24, pixels), F32),
            pltpu.VMEM((2, padded, channels), F32),
            pltpu.VMEM((padded, channels), F32),
            pltpu.VMEM((padded, channels), F32),
            pltpu.VMEM((groups, part, channels), F32),
            pltpu.VMEM((2, groups, part, channels), BF16),
            pltpu.VMEM((2, padded, channels), F32),
            dma((tiles,)), dma((tiles,)), dma((tiles,)), dma((tiles,)),
            dma((2,)), dma((2,)), dma((2,)), dma((2,)),
            dma, dma,
            dma((groups,)), dma((groups,)), dma((groups,)), dma((groups,)), dma((groups,)), dma((groups,)),
        ],
        compiler_params=pltpu.CompilerParams(
            collective_id=0, has_side_effects=True, vmem_limit_bytes=40 * 1024 * 1024
        ),
        name="step",
    )(
        dest_tile.reshape(1, rows), pixel_bin, waves[0], target[0],
        conv_one.reshape(3, 3 * steps, channels), bias_one.reshape(1, channels), conv_two, bias_two,
    )
    return pred[None], one, bias[0], two


def solution(mesh):
    placed = (
        P("rep", "tile", None),
        P("rep", "tile", None),
        P("rep", "tile"),
        P("rep", "tile", None),
        P(),
        P(),
        P(),
        P(),
    )
    return jax.shard_map(
        functools.partial(on_device, mesh.shape["tile"], mesh.shape["rep"]),
        mesh=mesh,
        in_specs=placed,
        out_specs=(P("rep", "tile", None), P(), P(), P()),
        check_vma=False,
    )
```

time: 187 us -> 44.9 us (0.24)
  blocking collectives: 71.8 us -> 0 us
  Pallas kernels: 0 us -> 37.6 us
  waiting for transfers between devices: 27 us -> 0 us
  starting transfers between devices: 24.4 us -> 0 us
  other arithmetic: 18.6 us -> 0 us
  between operations: 17.3 us -> 1.35 us
  local copies, waits for them, and re-layouts: 16.4 us -> 5.72 us
  matrix products: 10.1 us -> 0 us
    psum x2 -> x0, blocking collectives: 46.3 us -> none  [the longest x1 39.3 us: on_device(): grad_bias, grad_two = lax.psum((grad_bias, grad_two), ('tile', 'rep'))]
    pallas_call x0 -> x1, Pallas kernels: none -> 37.6 us  [on_device(): pl.pallas_call(functools.partial(step_kernel, tiles, reps, part), out_sha...]
    all_gather x1 -> x0, blocking collectives: 25.5 us -> none  [on_device(): lax.all_gather(share, 'tile', axis=0, tiled=True)]
    ppermute x6 -> x0, starting transfers between devices: 13 us -> none  [the longest x3 7.12 us: extended(): lax.ppermute(lax.slice_in_dim(block, 0, width, axis=dim), axis, backward)]
    all_to_all x2 -> x0, starting transfers between devices: 11.3 us -> none  [the longest x1 7.32 us: on_device(): lax.all_to_all(send_bin.reshape(tiles, bucket), 'tile', split_axis=0, con...]
    all_to_all x2 -> x0, waiting for transfers between devices: 10.2 us -> none  [the longest x1 6.81 us: on_device(): lax.all_to_all(send_wave.reshape(tiles, bucket, steps), 'tile', split_axi...]
    dot_general x44 -> x0, matrix products: 10.1 us -> none  [the longest x9 2.79 us: first_conv(): jnp.dot(patch, conv_one[i, j], preferred_element_type=jnp.float32)]
    unnamed x2 -> x0, waiting for transfers between devices: 8.45 us -> none
  transfers between devices with their start and end apart: 9 -> 0, of which waited for: 6 -> 0; matrix products, arithmetic and copies ran while one was open for 4% -> 0% of each run, Pallas kernels for 0% -> 0%
where the time goes in v1:
time: 44.9 us; the launch traced here: 44.7 us
  Pallas kernels  37.6 us (84%)
  local copies, waits for them, and re-layouts  5.72 us (13%)
  between operations  1.35 us (3%)
    pallas_call x1, Pallas kernels, on_device(): pl.pallas_call(functools.partial(step_kernel, tiles, reps, part), out_sha...  37.6 us
    unnamed x18, local copies, waits for them, and re-layouts  5.72 us

profile of v1, /device:TPU:1, one launch (start us, length us, event | category | flops | bytes accessed | tf_op | source)
XLA Modules:
  0.0 44.7 jit_solution(14786176048750619421)
XLA Ops:
  0.6 0.0 copy-start.5
  1.3 0.0 copy-start.4
  1.3 0.0 copy-start.2
  1.3 0.0 copy-start.3
  1.3 0.0 copy-done.5
  1.3 0.6 %copy-done.4 = s32[1,512,1]{1,2,0:T(1,128)S(1)} copy-done((s32[1,512,1]{1,2,0:T(1,128)S(1)}, s32[1,512,1]{1,2,0:T(1,128)}, u32[]{:S(2)}) %copy-start.4) | copy-done | bytes 2072
  2.0 0.0 copy-done.2
  2.0 0.0 copy-done.3
  2.0 0.0 copy-start
  2.0 1.0 %copy-done = bf16[3,3,128,128]{3,2,1,0:T(8,128)(2,1)S(1)} copy-done((bf16[3,3,128,128]{3,2,1,0:T(8,128)(2,1)S(1)}, bf16[3,3,128,128]{3,2,1,0:T(8,128)(2,1)}, u32[]{:S(2)}) %copy-start) | copy-done | bytes 294936
  3.0 0.0 copy-start.1
  3.0 0.9 %copy-done.1 = bf16[1,512,128]{2,1,0:T(8,128)(2,1)S(1)} copy-done((bf16[1,512,128]{2,1,0:T(8,128)(2,1)S(1)}, bf16[1,512,128]{2,1,0:T(8,128)(2,1)}, u32[]{:S(2)}) %copy-start.1) | copy-done | bytes 131096
  3.9 0.0 copy-start.6
  3.9 0.7 %copy-done.6 = f32[128]{0:T(128)S(1)} copy-done((f32[128]{0:T(128)S(1)}, f32[128]{0:T(128)}, u32[]{:S(2)}) %copy-start.6) | copy-done | bytes 536
  4.5 37.6 %step.1 = (f32[8,128]{1,0:T(8,128)S(1)}, f32[3,3,128,128]{3,2,1,0:T(8,128)S(1)}, f32[1,128]{1,0:T(1,128)S(1)}, f32[3,3,128]{2,1,0:T(4,128)S(1)}) custom-call(s32[1,512]{1,0:T(1,128)S(1)} %bitcast.11, s32[1,512]{1,0:T(1,128)S(1)} %copy-done.5, bf16[512,128]{1,0:T(8,128)(2,1)S(1)} %bitcast.8, f32[8,128]{1,0:T(8,128)S(1)} %bitcast.9, ...), custom_call_target="tpu_custom_call" | custom-call | tf_op jit(solution)/shard_map/step/pallas_call | solution.py:436
  42.2 0.6 %copy.17 = f32[1,8,128]{2,1,0:T(8,128)} copy(f32[1,8,128]{2,1,0:T(8,128)S(1)} %bitcast.10) | data formatting | bytes 8192
  42.8 0.8 %copy.18 = f32[3,3,128,128]{3,2,1,0:T(8,128)} copy(f32[3,3,128,128]{3,2,1,0:T(8,128)S(1)} %get-tuple-element.17) | data formatting | bytes 1179648
  43.6 0.5 %copy.19 = f32[128]{0:T(128)} copy(f32[128]{0:T(128)S(1)} %bitcast.13) | data formatting | bytes 1024
  44.1 0.6 %copy.20 = f32[3,3,128]{2,1,0:T(4,128)} copy(f32[3,3,128]{2,1,0:T(4,128)S(1)} %get-tuple-element.19) | data formatting | bytes 9216
Async XLA Ops:
  0.6 0.7 %copy-start.5 = (s32[1,512]{1,0:T(1,128)S(1)}, s32[1,512]{1,0:T(1,128)}, u32[]{:S(2)}) copy-start(s32[1,512]{1,0:T(1,128)} %bin_ref.1) | copy-start | bytes 6148
  1.3 0.7 %copy-start.4 = (s32[1,512,1]{1,2,0:T(1,128)S(1)}, s32[1,512,1]{1,2,0:T(1,128)}, u32[]{:S(2)}) copy-start(s32[1,512,1]{1,2,0:T(1,128)} %param.9) | copy-start | bytes 6148
  1.3 0.7 %copy-start.2 = (f32[1,8,128]{2,1,0:T(8,128)S(1)}, f32[1,8,128]{2,1,0:T(8,128)}, u32[]{:S(2)}) copy-start(f32[1,8,128]{2,1,0:T(8,128)} %param.11) | copy-start | bytes 12292
  1.3 0.7 %copy-start.3 = (bf16[3,3,128]{2,1,0:T(4,128)(2,1)S(1)}, bf16[3,3,128]{2,1,0:T(4,128)(2,1)}, u32[]{:S(2)}) copy-start(bf16[3,3,128]{2,1,0:T(4,128)(2,1)} %w2_ref.1) | copy-start | bytes 6916
  2.0 1.0 %copy-start = (bf16[3,3,128,128]{3,2,1,0:T(8,128)(2,1)S(1)}, bf16[3,3,128,128]{3,2,1,0:T(8,128)(2,1)}, u32[]{:S(2)}) copy-start(bf16[3,3,128,128]{3,2,1,0:T(8,128)(2,1)} %param.12) | copy-start | bytes 884740
  3.0 0.9 %copy-start.1 = (bf16[1,512,128]{2,1,0:T(8,128)(2,1)S(1)}, bf16[1,512,128]{2,1,0:T(8,128)(2,1)}, u32[]{:S(2)}) copy-start(bf16[1,512,128]{2,1,0:T(8,128)(2,1)} %param.8) | copy-start | bytes 393220
  3.9 0.7 %copy-start.6 = (f32[128]{0:T(128)S(1)}, f32[128]{0:T(128)}, u32[]{:S(2)}) copy-start(f32[128]{0:T(128)} %param.13) | copy-start | bytes 1540

commit v2 on v1

--- a/solution.py
+++ b/solution.py
@@ -24,12 +24,13 @@
 
 def step_kernel(
     tiles, reps, part,
-    dest_ref, bin_ref, waves_ref, target_ref, w1_ref, b1_ref, w2_ref, b2_ref,
-    pred_ref, u1_ref, ub_ref, u2_ref,
+    dest_hbm, bin_hbm, waves_hbm, target_hbm, w1_hbm, b1_hbm, w2_hbm, b2_hbm,
+    pred_ref, out_ref,
+    dest_ref, bin_ref, waves_ref, target_ref, w1_ref, b1_ref, w2_ref, b2_ref, l_sem,
     sendw, sendb, recvw, recvb, grid, wide, pre_s, hid_s, tlow, thigh, w2_s, taps, etap,
-    full, pair, total, recvs, gathered, flat,
+    full, pair, total, recva, recvs, gathered,
     aw_send, aw_recv, ab_send, ab_recv, t_send, t_recv, g_send, g_recv,
-    p_send, p_recv, r_send, r_recv, n_send, n_recv, f_send, f_recv,
+    p_send, p_recv, s_send, s_recv, r_send, r_recv, n_send, n_recv, f_send, f_recv,
 ):
     me = lax.axis_index("tile")
     rep = lax.axis_index("rep")
@@ -38,9 +39,13 @@
     channels = b1_ref.shape[1]
     half = tiles // 2
     groups = half * reps
+    outer, inner = split(tiles, reps)
+    minor = outer // reps
     core = lax.rem(me, 2)
     partner = me + 1 - 2 * core
-    chip = rep * half + me // 2
+    at_outer = rep * minor + lax.rem(me // 2, minor)
+    at_inner = me // 2 // minor
+    chip = at_outer * inner + at_inner
     pixels = height * width
     tall = height + HALO
 
@@ -49,7 +54,10 @@
 
     def group_peer(k):
         q = lax.rem(chip + k, groups)
-        return q, {"tile": 2 * lax.rem(q, half) + core, "rep": q // half}
+        return q, device_at(q // inner, lax.rem(q, inner))
+
+    def device_at(a, b):
+        return {"tile": 2 * (b * minor + lax.rem(a, minor)) + core, "rep": a // minor}
 
     barrier = pltpu.get_barrier_semaphore()
 
@@ -69,6 +77,20 @@
         return carry
 
     lax.fori_loop(0, (reps - 1) * half, greet_far, 0)
+
+    loads = [
+        pltpu.make_async_copy(src, dst, l_sem.at[k])
+        for k, (src, dst) in enumerate(
+            [
+                (dest_hbm, dest_ref), (bin_hbm, bin_ref), (waves_hbm, waves_ref), (target_hbm, target_ref),
+                (w1_hbm, w1_ref), (b1_hbm, b1_ref), (w2_hbm, w2_ref), (b2_hbm, b2_ref),
+            ]
+        )
+    ]
+    for load in loads:
+        load.start()
+    for load in loads[:4]:
+        load.wait()
 
     hits = (iota((tiles, rows), 0) == dest_ref[...]).astype(F32)
     earlier = (iota((rows, rows), 0) < iota((rows, rows), 1)).astype(F32).astype(BF16)
@@ -163,6 +185,8 @@
     own = pl.ds(pl.multiple_of(me * CAP, CAP), CAP)
     recvw[own, :] = sendw[own, :]
     recvb[me] = sendb[me]
+    for load in loads[4:]:
+        load.wait()
     w2_s[...] = jnp.zeros(w2_s.shape, F32)
     for i in range(3):
         w2_s[8 * i : 8 * i + 3, :] = w2_ref[i].astype(F32)
@@ -209,19 +233,9 @@
     for y in range(HALO, HALO + height):
         spread(y)
 
-    @pl.when(has_down)
-    def _():
-        grid_up.wait_recv()
-
-    @pl.when(has_up)
-    def _():
-        grid_down.wait_recv()
-
-    for y in list(range(HALO)) + list(range(HALO + height, 2 * HALO + height)):
-        spread(y)
-
     bias = b1_ref[...]
-    for y in range(0, tall, 2):
+
+    def convolve(y):
         acc = jnp.zeros((2 * width, channels), F32) + bias
         for i in range(3):
             acc = acc + dot(wide[(y + 2 * i) * width : (y + 2 * i + 2) * width, :], w1_ref[i])
@@ -234,6 +248,25 @@
         hid_s[y * width : (y + 2) * width, :] = hidden.astype(BF16)
         if 2 <= y < height + 2:
             pre_s[(y - 2) * width : y * width, :] = sig * (1.0 + acc * (1.0 - sig))
+
+    middle = [y for y in range(HALO, height, 2)]
+    for y in middle:
+        convolve(y)
+
+    @pl.when(has_down)
+    def _():
+        grid_up.wait_recv()
+
+    @pl.when(has_up)
+    def _():
+        grid_down.wait_recv()
+
+    for y in list(range(HALO)) + list(range(HALO + height, 2 * HALO + height)):
+        spread(y)
+
+    for y in range(0, tall, 2):
+        if y not in middle:
+            convolve(y)
 
     each = dot(w2, hid_s[...], ((1,), (1,)))
     span2 = (height + 2) * width
@@ -292,6 +325,17 @@
         full[h, small + 24 : small + 32, :] = grad_bias
         if full.shape[1] > small + 32:
             full[h, small + 32 :, :] = jnp.zeros((full.shape[1] - small - 32, channels), F32)
+    slab = inner * part
+
+    def swap(a):
+        rows_a = pl.ds(a * slab, slab)
+        return pltpu.make_async_remote_copy(
+            src_ref=full.at[1 - core, rows_a], dst_ref=pair.at[rows_a],
+            send_sem=p_send.at[a], recv_sem=p_recv.at[a],
+            device_id={"tile": partner, "rep": rep}, device_id_type=MESH,
+        )
+
+    started = 0
     for i in range(3):
         start = (2 + 2 * i) * width
         g = dot(wide[start : start + pixels, :], slope, ((0,), (0,)))
@@ -299,37 +343,64 @@
             k = 3 * i + j
             for h in range(2):
                 full[h, k * piece : (k + 1) * piece, :] = g[j * steps + h * piece : j * steps + (h + 1) * piece, :]
-
-    swap = pltpu.make_async_remote_copy(
-        src_ref=full.at[1 - core], dst_ref=pair, send_sem=p_send, recv_sem=p_recv,
-        device_id={"tile": partner, "rep": rep}, device_id_type=MESH,
-    )
-    swap.start()
-    swap.wait_recv()
-    total[...] = full[core] + pair[...]
-
-    def share_copy(q, device, source):
-        return pltpu.make_async_remote_copy(
-            src_ref=total.at[pl.ds(pl.multiple_of(q * part, 8), part)], dst_ref=recvs.at[source],
-            send_sem=r_send.at[q], recv_sem=r_recv.at[source], device_id=device, device_id_type=MESH,
-        )
-
-    def give(k, carry):
-        q, device = group_peer(k)
-        share_copy(q, device, chip).start()
-        return carry
-
-    lax.fori_loop(1, groups, give, 0)
-    recvs[chip] = total[pl.ds(pl.multiple_of(chip * part, 8), part), :]
-
-    def take(k, carry):
-        q, device = group_peer(k)
-        share_copy(q, device, q).wait_recv()
-        return carry
-
-    lax.fori_loop(1, groups, take, 0)
-    share = lax.fori_loop(1, groups, lambda q, acc: acc + recvs[q], recvs[0])
-    gathered[core, chip] = share.astype(BF16)
+        while started < outer and ((started + 1) * slab <= 3 * (i + 1) * piece or i == 2):
+            swap(started).start()
+            started += 1
+
+    def slab_copy(a, source):
+        return pltpu.make_async_remote_copy(
+            src_ref=total.at[pl.ds(a * slab, slab)], dst_ref=recva.at[source],
+            send_sem=s_send.at[a], recv_sem=s_recv.at[source],
+            device_id=device_at(a, at_inner), device_id_type=MESH,
+        )
+
+    for a in range(outer):
+        swap(a).wait_recv()
+        rows_a = slice(a * slab, (a + 1) * slab)
+        total[rows_a, :] = full[core, rows_a, :] + pair[rows_a, :]
+
+        @pl.when(at_outer != a)
+        def _():
+            slab_copy(a, at_outer).start()
+
+    recva[at_outer] = total[pl.ds(pl.multiple_of(at_outer * slab, 8), slab), :]
+    for a in range(outer):
+
+        @pl.when(at_outer != a)
+        def _():
+            slab_copy(a, a).wait_recv()
+
+    plane = recva[0]
+    for a in range(1, outer):
+        plane = plane + recva[a]
+    pair[0:slab, :] = plane
+
+    def share_copy(b, source):
+        return pltpu.make_async_remote_copy(
+            src_ref=pair.at[pl.ds(b * part, part)], dst_ref=recvs.at[source],
+            send_sem=r_send.at[b], recv_sem=r_recv.at[source],
+            device_id=device_at(at_outer, b), device_id_type=MESH,
+        )
+
+    for b in range(inner):
+
+        @pl.when(at_inner != b)
+        def _():
+            share_copy(b, at_inner).start()
+
+    recvs[at_inner] = pair[pl.ds(pl.multiple_of(at_inner * part, 8), part), :]
+    for b in range(inner):
+
+        @pl.when(at_inner != b)
+        def _():
+            share_copy(b, b).wait_recv()
+
+    share = recvs[0]
+    for b in range(1, inner):
+        share = share + recvs[b]
+    rest = share - share.astype(BF16).astype(F32)
+    tail = jnp.logical_and(iota(share.shape, 0) + chip * part >= small, core == 1)
+    gathered[core, chip] = jnp.where(tail, rest, share).astype(BF16)
 
     def spread_copy(device, source):
         return pltpu.make_async_remote_copy(
@@ -370,22 +441,7 @@
 
     lax.fori_loop(0, groups, finish, 0)
 
-    def normalized(g, count, sums):
-        return g / jnp.sqrt(sums / count + 1e-06)
-
-    for h in range(2):
-        flat[h] = gathered[h].astype(F32).reshape(groups * part, channels)
-    one = flat[:, 0:small, :]
-    scale = jnp.sqrt(jnp.sum(one * one) / (9 * steps * channels) + 1e-06)
-    for k in range(9):
-        for h in range(2):
-            u1_ref[k // 3, k % 3, h * piece : (h + 1) * piece, :] = flat[h, k * piece : (k + 1) * piece, :] / scale
-    two = flat[0, small : small + 24, :]
-    two = two / jnp.sqrt(jnp.sum(two * two) / (9 * channels) + 1e-06)
-    for i in range(3):
-        u2_ref[i] = two[8 * i : 8 * i + 3, :]
-    gb = flat[0, small + 24 : small + 25, :]
-    ub_ref[...] = gb / jnp.sqrt(jnp.sum(gb * gb) / channels + 1e-06)
+    out_ref[...] = gathered[...]
 
     @pl.when(has_up)
     def _():
@@ -404,11 +460,22 @@
         return carry
 
     lax.fori_loop(1, tiles, sent, 0)
-    swap.wait_send()
+    for a in range(outer):
+        swap(a).wait_send()
+
+        @pl.when(at_outer != a)
+        def _():
+            slab_copy(a, at_outer).wait_send()
+
+    for b in range(inner):
+
+        @pl.when(at_inner != b)
+        def _():
+            share_copy(b, at_inner).wait_send()
+
 
     def shared(k, carry):
         q, device = group_peer(k)
-        share_copy(q, device, chip).wait_send()
         spread_copy(device, q).wait_send()
         return carry
 
@@ -419,6 +486,44 @@
         return carry
 
     lax.fori_loop(0, groups, passed, 0)
+
+
+def finish_kernel(
+    pred_ref, gathered, pred_out, u1_out, ub_out, u2_out, flat, u1, ub, u2, sem
+):
+    groups, part, channels = gathered.shape[1:]
+    steps = u1.shape[2]
+    piece = steps // 2
+    small = 9 * piece
+    copies = [
+        pltpu.make_async_copy(src, dst, sem.at[k])
+        for k, (src, dst) in enumerate([(pred_ref, pred_out), (u1, u1_out), (ub, ub_out), (u2, u2_out)])
+    ]
+    copies[0].start()
+    for h in range(2):
+        flat[h] = gathered[h].astype(F32).reshape(groups * part, channels)
+    one = flat[:, 0:small, :]
+    scale = 1.0 / jnp.sqrt(jnp.sum(one * one) / (9 * steps * channels) + 1e-06)
+    for k in range(9):
+        for h in range(2):
+            u1[k // 3, k % 3, h * piece : (h + 1) * piece, :] = flat[h, k * piece : (k + 1) * piece, :] * scale
+    copies[1].start()
+    two = flat[0, small : small + 24, :] + flat[1, small : small + 24, :]
+    two = two / jnp.sqrt(jnp.sum(two * two) / (9 * channels) + 1e-06)
+    for i in range(3):
+        u2[i] = two[8 * i : 8 * i + 3, :]
+    gb = flat[0, small + 24 : small + 25, :] + flat[1, small + 24 : small + 25, :]
+    ub[...] = gb / jnp.sqrt(jnp.sum(gb * gb) / channels + 1e-06)
+    copies[2].start()
+    copies[3].start()
+    for copy in copies:
+        copy.wait()
+
+
+def split(tiles, reps):
+    half = tiles // 2
+    minor = 2 if half % 2 == 0 else 1
+    return reps * minor, half // minor
 
 
 def on_device(tiles, reps, waves, dest_tile, pixel_bin, target, conv_one, bias_one, conv_two, bias_two):
@@ -430,20 +535,29 @@
     small = 9 * (steps // 2)
     part = -(-(small + 32) // (8 * groups)) * 8
     padded = groups * part
+    outer, inner = split(tiles, reps)
+    hbm = pl.BlockSpec(memory_space=pltpu.HBM)
     tp = -(-(height + 2) // 8) * 8
     dma = pltpu.SemaphoreType.DMA
     vmem = pl.BlockSpec(memory_space=pltpu.VMEM)
-    pred, one, bias, two = pl.pallas_call(
+    pred, gathered = pl.pallas_call(
         functools.partial(step_kernel, tiles, reps, part),
         out_shape=(
             jax.ShapeDtypeStruct((height, width), F32),
-            jax.ShapeDtypeStruct((3, 3, steps, channels), F32),
-            jax.ShapeDtypeStruct((1, channels), F32),
-            jax.ShapeDtypeStruct((3, 3, channels), F32),
+            jax.ShapeDtypeStruct((2, groups, part, channels), BF16),
         ),
-        in_specs=[vmem] * 7 + [pl.BlockSpec(memory_space=pltpu.SMEM)],
-        out_specs=(vmem,) * 4,
+        in_specs=[hbm] * 8,
+        out_specs=(vmem,) * 2,
         scratch_shapes=[
+            pltpu.VMEM((1, rows), jnp.int32),
+            pltpu.VMEM((1, rows), jnp.int32),
+            pltpu.VMEM((rows, steps), BF16),
+            pltpu.VMEM((height, width), F32),
+            pltpu.VMEM((3, 3 * steps, channels), BF16),
+            pltpu.VMEM((1, channels), F32),
+            pltpu.VMEM((3, 3, channels), BF16),
+            pltpu.SMEM((1,), F32),
+            dma((8,)),
             pltpu.VMEM((tiles * CAP, steps), BF16),
             pltpu.VMEM((tiles, 1, 128), F32),
             pltpu.VMEM((tiles * CAP, steps), BF16),
@@ -460,13 +574,13 @@
             pltpu.VMEM((2, padded, channels), F32),
             pltpu.VMEM((padded, channels), F32),
             pltpu.VMEM((padded, channels), F32),
-            pltpu.VMEM((groups, part, channels), F32),
+            pltpu.VMEM((outer, inner * part, channels), F32),
+            pltpu.VMEM((inner, part, channels), F32),
             pltpu.VMEM((2, groups, part, channels), BF16),
-            pltpu.VMEM((2, padded, channels), F32),
             dma((tiles,)), dma((tiles,)), dma((tiles,)), dma((tiles,)),
             dma((2,)), dma((2,)), dma((2,)), dma((2,)),
-            dma, dma,
-            dma((groups,)), dma((groups,)), dma((groups,)), dma((groups,)), dma((groups,)), dma((groups,)),
+            dma((outer,)), dma((outer,)), dma((outer,)), dma((outer,)), dma((inner,)), dma((inner,)),
+            dma((groups,)), dma((groups,)), dma((groups,)), dma((groups,)),
         ],
         compiler_params=pltpu.CompilerParams(
             collective_id=0, has_side_effects=True, vmem_limit_bytes=40 * 1024 * 1024
@@ -476,6 +590,25 @@
         dest_tile.reshape(1, rows), pixel_bin, waves[0], target[0],
         conv_one.reshape(3, 3 * steps, channels), bias_one.reshape(1, channels), conv_two, bias_two,
     )
+    pred, one, bias, two = pl.pallas_call(
+        finish_kernel,
+        out_shape=(
+            jax.ShapeDtypeStruct((height, width), F32),
+            jax.ShapeDtypeStruct((3, 3, steps, channels), F32),
+            jax.ShapeDtypeStruct((1, channels), F32),
+            jax.ShapeDtypeStruct((3, 3, channels), F32),
+        ),
+        in_specs=[vmem] * 2,
+        out_specs=(hbm,) * 4,
+        scratch_shapes=[
+            pltpu.VMEM((2, padded, channels), F32),
+            pltpu.VMEM((3, 3, steps, channels), F32),
+            pltpu.VMEM((1, channels), F32),
+            pltpu.VMEM((3, 3, channels), F32),
+            dma((4,)),
+        ],
+        name="finish",
+    )(pred, gathered)
     return pred[None], one, bias[0], two
 
 

time: 44.9 us -> 45.5 us (1.013)
  Pallas kernels: 37.6 us -> 39.4 us
  local copies, waits for them, and re-layouts: 5.72 us -> 4.51 us
    pallas_call x0 -> x1, Pallas kernels: none -> 2.28 us  [on_device(): pl.pallas_call(finish_kernel, out_shape=(jax.ShapeDtypeStruct((height, wi...]
    unnamed x18, local copies, waits for them, and re-layouts: 5.72 us -> 4.51 us
    pallas_call x1, Pallas kernels: 37.6 us -> 37.1 us  [on_device(): pl.pallas_call(functools.partial(step_kernel, tiles, reps, part), out_sha...]
where the time goes in v2:
time: 45.5 us; the launch traced here: 45.2 us
  Pallas kernels  39.4 us (87%)
  local copies, waits for them, and re-layouts  4.51 us (10%)
  between operations  1.35 us (3%)
    pallas_call x1, Pallas kernels, on_device(): pl.pallas_call(functools.partial(step_kernel, tiles, reps, part), out_sha...  37.1 us
    unnamed x18, local copies, waits for them, and re-layouts  4.51 us
    pallas_call x1, Pallas kernels, on_device(): pl.pallas_call(finish_kernel, out_shape=(jax.ShapeDtypeStruct((height, wi...  2.28 us

profile of v2, /device:TPU:1, one launch (start us, length us, event | category | flops | bytes accessed | tf_op | source)
XLA Modules:
  0.0 45.2 jit_solution(4621206922354595002)
XLA Ops:
  0.6 0.0 copy-start.7
  1.3 0.0 copy-start.6
  1.3 0.0 copy-start.3
  1.3 0.0 copy-start.5
  1.3 0.0 copy-done.7
  1.3 0.6 %copy-done.6 = s32[1,512,1]{1,2,0:T(1,128)S(1)} copy-done((s32[1,512,1]{1,2,0:T(1,128)S(1)}, s32[1,512,1]{1,2,0:T(1,128)}, u32[]{:S(2)}) %copy-start.6) | copy-done | bytes 2072
  2.0 0.0 copy-done.3
  2.0 0.0 copy-done.5
  2.0 0.0 copy-start.1
  2.0 1.0 %copy-done.1 = bf16[3,3,128,128]{3,2,1,0:T(8,128)(2,1)S(1)} copy-done((bf16[3,3,128,128]{3,2,1,0:T(8,128)(2,1)S(1)}, bf16[3,3,128,128]{3,2,1,0:T(8,128)(2,1)}, u32[]{:S(2)}) %copy-start.1) | copy-done | bytes 294936
  3.0 0.0 copy-start.2
  3.0 0.9 %copy-done.2 = bf16[1,512,128]{2,1,0:T(8,128)(2,1)S(1)} copy-done((bf16[1,512,128]{2,1,0:T(8,128)(2,1)S(1)}, bf16[1,512,128]{2,1,0:T(8,128)(2,1)}, u32[]{:S(2)}) %copy-start.2) | copy-done | bytes 131096
  3.9 0.0 copy-start.8
  3.9 0.7 %copy-done.8 = f32[128]{0:T(128)S(1)} copy-done((f32[128]{0:T(128)S(1)}, f32[128]{0:T(128)}, u32[]{:S(2)}) %copy-start.8) | copy-done | bytes 536
  4.5 37.1 %step.1 = (f32[8,128]{1,0:T(8,128)S(1)}, bf16[2,16,40,128]{3,2,1,0:T(8,128)(2,1)S(1)}) custom-call(s32[1,512]{1,0:T(1,128)S(1)} %bitcast.10, s32[1,512]{1,0:T(1,128)S(1)} %copy-done.7, bf16[512,128]{1,0:T(8,128)(2,1)S(1)} %bitcast.8, f32[8,128]{1,0:T(8,128)S(1)} %bitcast.9, bf16[3,384,128]{2,1,0:T(8,128)(2,1)S(1)} %bitcast.7, f32[1,128]{1,0:T(1,128)S(1)} %bitcast.11, ...), custom_call_target="tpu_custom_call" | custom-call | tf_op jit(solution)/shard_map/step/pallas_call | solution.py:543
  41.7 0.0 copy-start
  41.7 0.7 %copy-done = bf16[2,16,40,128]{3,2,1,0:T(8,128)(2,1)} copy-done((bf16[2,16,40,128]{3,2,1,0:T(8,128)(2,1)}, bf16[2,16,40,128]{3,2,1,0:T(8,128)(2,1)S(1)}, u32[]{:S(2)}) %copy-start) | copy-done | bytes 327704
  42.4 0.0 copy-start.4
  42.4 0.6 %copy-done.4 = f32[8,128]{1,0:T(8,128)} copy-done((f32[8,128]{1,0:T(8,128)}, f32[8,128]{1,0:T(8,128)S(1)}, u32[]{:S(2)}) %copy-start.4) | copy-done | bytes 4120
  43.0 2.3 %finish.1 = (f32[8,128]{1,0:T(8,128)}, f32[3,3,128,128]{3,2,1,0:T(8,128)}, f32[1,128]{1,0:T(1,128)}, f32[3,3,128]{2,1,0:T(4,128)}) custom-call(f32[8,128]{1,0:T(8,128)} %copy-done.4, bf16[2,16,40,128]{3,2,1,0:T(8,128)(2,1)} %copy-done), custom_call_target="tpu_custom_call" | custom-call | tf_op jit(solution)/shard_map/finish/pallas_call | solution.py:593
Async XLA Ops:
  0.6 0.7 %copy-start.7 = (s32[1,512]{1,0:T(1,128)S(1)}, s32[1,512]{1,0:T(1,128)}, u32[]{:S(2)}) copy-start(s32[1,512]{1,0:T(1,128)} %bin_hbm.1) | copy-start | bytes 6148
  1.3 0.7 %copy-start.6 = (s32[1,512,1]{1,2,0:T(1,128)S(1)}, s32[1,512,1]{1,2,0:T(1,128)}, u32[]{:S(2)}) copy-start(s32[1,512,1]{1,2,0:T(1,128)} %param.9) | copy-start | bytes 6148
  1.3 0.7 %copy-start.3 = (f32[1,8,128]{2,1,0:T(8,128)S(1)}, f32[1,8,128]{2,1,0:T(8,128)}, u32[]{:S(2)}) copy-start(f32[1,8,128]{2,1,0:T(8,128)} %param.11) | copy-start | bytes 12292
  1.3 0.7 %copy-start.5 = (bf16[3,3,128]{2,1,0:T(4,128)(2,1)S(1)}, bf16[3,3,128]{2,1,0:T(4,128)(2,1)}, u32[]{:S(2)}) copy-start(bf16[3,3,128]{2,1,0:T(4,128)(2,1)} %w2_hbm.1) | copy-start | bytes 6916
  2.0 1.0 %copy-start.1 = (bf16[3,3,128,128]{3,2,1,0:T(8,128)(2,1)S(1)}, bf16[3,3,128,128]{3,2,1,0:T(8,128)(2,1)}, u32[]{:S(2)}) copy-start(bf16[3,3,128,128]{3,2,1,0:T(8,128)(2,1)} %param.12) | copy-start | bytes 884740
  3.0 0.9 %copy-start.2 = (bf16[1,512,128]{2,1,0:T(8,128)(2,1)S(1)}, bf16[1,512,128]{2,1,0:T(8,128)(2,1)}, u32[]{:S(2)}) copy-start(bf16[1,512,128]{2,1,0:T(8,128)(2,1)} %param.8) | copy-start | bytes 393220
  3.9 0.7 %copy-start.8 = (f32[128]{0:T(128)S(1)}, f32[128]{0:T(128)}, u32[]{:S(2)}) copy-start(f32[128]{0:T(128)} %param.13) | copy-start | bytes 1540
  41.7 0.7 %copy-start = (bf16[2,16,40,128]{3,2,1,0:T(8,128)(2,1)}, bf16[2,16,40,128]{3,2,1,0:T(8,128)(2,1)S(1)}, u32[]{:S(2)}) copy-start(bf16[2,16,40,128]{3,2,1,0:T(8,128)(2,1)S(1)} %get-tuple-element.11.gathered) | copy-start | bytes 983044
  42.4 0.6 %copy-start.4 = (f32[8,128]{1,0:T(8,128)}, f32[8,128]{1,0:T(8,128)S(1)}, u32[]{:S(2)}) copy-start(f32[8,128]{1,0:T(8,128)S(1)} %get-tuple-element.10.pred_ref) | copy-start | bytes 12292

commit v3 on v2

--- a/solution.py
+++ b/solution.py
@@ -583,7 +583,7 @@
             dma((groups,)), dma((groups,)), dma((groups,)), dma((groups,)),
         ],
         compiler_params=pltpu.CompilerParams(
-            collective_id=0, has_side_effects=True, vmem_limit_bytes=40 * 1024 * 1024
+            collective_id=0, has_side_effects=True, vmem_limit_bytes=60 * 1024 * 1024
         ),
         name="step",
     )(

time: 45.5 us -> 41.9 us (0.921)
  local copies, waits for them, and re-layouts: 4.51 us -> 0 us
  Pallas kernels: 39.4 us -> 40.4 us
    unnamed x18 -> x0, local copies, waits for them, and re-layouts: 4.51 us -> none
    pallas_call x1, Pallas kernels: 37.1 us -> 38.1 us  [on_device(): pl.pallas_call(functools.partial(step_kernel, tiles, reps, part), out_sha...]
where the time goes in v3:
time: 41.9 us; the launch traced here: 41.7 us
  Pallas kernels  40.4 us (96%)
  between operations  1.29 us (3%)
    pallas_call x1, Pallas kernels, on_device(): pl.pallas_call(functools.partial(step_kernel, tiles, reps, part), out_sha...  38.1 us
    pallas_call x1, Pallas kernels, on_device(): pl.pallas_call(finish_kernel, out_shape=(jax.ShapeDtypeStruct((height, wi...  2.28 us

profile of v3, /device:TPU:1, one launch (start us, length us, event | category | flops | bytes accessed | tf_op | source)
XLA Modules:
  0.0 41.7 jit_solution(9730589843016616664)
XLA Ops:
  1.3 38.1 %step.1 = (f32[8,128]{1,0:T(8,128)}, bf16[2,16,40,128]{3,2,1,0:T(8,128)(2,1)}) custom-call(s32[1,512]{1,0:T(1,128)} %bitcast.10, s32[1,512]{1,0:T(1,128)} %bin_hbm.1, bf16[512,128]{1,0:T(8,128)(2,1)} %bitcast.8, f32[8,128]{1,0:T(8,128)} %bitcast.9, bf16[3,384,128]{2,1,0:T(8,128)(2,1)} %bitcast.7, f32[1,128]{1,0:T(1,128)} %bitcast.11, ...), custom_call_target="tpu_custom_call" | custom-call | tf_op jit(solution)/shard_map/step/pallas_call | solution.py:543
  39.4 2.3 %finish.1 = (f32[8,128]{1,0:T(8,128)}, f32[3,3,128,128]{3,2,1,0:T(8,128)}, f32[1,128]{1,0:T(1,128)}, f32[3,3,128]{2,1,0:T(4,128)}) custom-call(f32[8,128]{1,0:T(8,128)} %get-tuple-element.10.pred_ref, bf16[2,16,40,128]{3,2,1,0:T(8,128)(2,1)} %get-tuple-element.11.gathered), custom_call_target="tpu_custom_call" | custom-call | tf_op jit(solution)/shard_map/finish/pallas_call | solution.py:593

commit v4 on v3

--- a/solution.py
+++ b/solution.py
@@ -27,10 +27,10 @@
     dest_hbm, bin_hbm, waves_hbm, target_hbm, w1_hbm, b1_hbm, w2_hbm, b2_hbm,
     pred_ref, out_ref,
     dest_ref, bin_ref, waves_ref, target_ref, w1_ref, b1_ref, w2_ref, b2_ref, l_sem,
-    sendw, sendb, recvw, recvb, grid, wide, pre_s, hid_s, tlow, thigh, w2_s, taps, etap,
+    sendw, recvw, grid, wide, pre_s, hid_s, tlow, thigh, w2_s, taps, etap,
     full, pair, total, recva, recvs, gathered,
-    aw_send, aw_recv, ab_send, ab_recv, t_send, t_recv, g_send, g_recv,
-    p_send, p_recv, s_send, s_recv, r_send, r_recv, n_send, n_recv, f_send, f_recv,
+    aw_send, aw_recv, t_send, t_recv, g_send, g_recv,
+    p_send, p_recv, s_send, s_recv, r_send, r_recv, n_send, n_recv, m_send, m_recv, f_send, f_recv,
 ):
     me = lax.axis_index("tile")
     rep = lax.axis_index("rep")
@@ -52,10 +52,6 @@
     def tile_peer(k):
         return lax.rem(me + k, tiles)
 
-    def group_peer(k):
-        q = lax.rem(chip + k, groups)
-        return q, device_at(q // inner, lax.rem(q, inner))
-
     def device_at(a, b):
         return {"tile": 2 * (b * minor + lax.rem(a, minor)) + core, "rep": a // minor}
 
@@ -71,13 +67,15 @@
         pl.semaphore_signal(
             barrier,
             inc=1,
-            device_id={"tile": 2 * lax.rem(k, half) + core, "rep": lax.rem(rep + 1 + k // half, reps)},
+            device_id={
+                "tile": 2 * (at_inner * minor + lax.rem(k, minor)) + core,
+                "rep": lax.rem(rep + 1 + k // minor, reps),
+            },
             device_id_type=MESH,
         )
         return carry
 
-    lax.fori_loop(0, (reps - 1) * half, greet_far, 0)
-
+    lax.fori_loop(0, (reps - 1) * minor, greet_far, 0)
     loads = [
         pltpu.make_async_copy(src, dst, l_sem.at[k])
         for k, (src, dst) in enumerate(
@@ -98,44 +96,34 @@
     rank = jnp.sum(hits * ranks, axis=0, keepdims=True)
     slot = jnp.sum(hits * (ranks + (CAP * iota((tiles, rows), 0)).astype(F32)), axis=0, keepdims=True)
     place = (iota((tiles * CAP, rows), 0).astype(F32) == slot).astype(F32).astype(BF16)
-    sendw[...] = dot(place, waves_ref[...]).astype(BF16)
+    sendw[:, 0:CAP, :] = dot(place, waves_ref[...]).astype(BF16).reshape(tiles, CAP, steps)
     lane = rank + (CAP * lax.rem(me, 4)).astype(F32)
     lanes = (iota((128, rows), 0).astype(F32) == lane).astype(F32).astype(BF16)
     bins = bin_ref[...]
     high = (bins // 32).astype(F32)
     low = (bins - 32 * (bins // 32)).astype(F32)
-    named = 32.0 * dot((hits * high).astype(BF16), lanes, ((1,), (1,))) + dot(
-        (hits * low).astype(BF16), lanes, ((1,), (1,))
-    )
+    highs = dot((hits * high).astype(BF16), lanes, ((1,), (1,)))
+    lows = dot((hits * low).astype(BF16), lanes, ((1,), (1,)))
+    turn = iota((8, 128), 0)
     for t in range(tiles):
-        sendb[t] = named[t : t + 1, :]
-
-    pl.semaphore_wait(barrier, tiles - 1 + (reps - 1) * half)
+        both = jnp.where(turn == 0, highs[t : t + 1, :], jnp.where(turn == 1, lows[t : t + 1, :], 0.0))
+        sendw[t, CAP:, :] = both.astype(BF16)
+
+    pl.semaphore_wait(barrier, tiles - 1 + (reps - 1) * minor)
 
     def wave_copy(peer, source):
         return pltpu.make_async_remote_copy(
-            src_ref=sendw.at[pl.ds(pl.multiple_of(peer * CAP, CAP), CAP)],
-            dst_ref=recvw.at[pl.ds(pl.multiple_of(source * CAP, CAP), CAP)],
+            src_ref=sendw.at[peer],
+            dst_ref=recvw.at[source],
             send_sem=aw_send.at[peer],
             recv_sem=aw_recv.at[source],
             device_id={"tile": peer, "rep": rep},
             device_id_type=MESH,
         )
 
-    def bin_copy(peer, source):
-        return pltpu.make_async_remote_copy(
-            src_ref=sendb.at[peer],
-            dst_ref=recvb.at[source],
-            send_sem=ab_send.at[peer],
-            recv_sem=ab_recv.at[source],
-            device_id={"tile": peer, "rep": rep},
-            device_id_type=MESH,
-        )
-
     def scatter(k, carry):
         peer = tile_peer(k)
         wave_copy(peer, me).start()
-        bin_copy(peer, me).start()
         return carry
 
     lax.fori_loop(1, tiles, scatter, 0)
@@ -182,9 +170,7 @@
         grid[span + pixels : span + pixels + span, :] = jnp.zeros((span, steps), BF16)
         thigh[...] = jnp.zeros((height, width), F32)
 
-    own = pl.ds(pl.multiple_of(me * CAP, CAP), CAP)
-    recvw[own, :] = sendw[own, :]
-    recvb[me] = sendb[me]
+    recvw[me] = sendw[me]
     for load in loads[4:]:
         load.wait()
     w2_s[...] = jnp.zeros(w2_s.shape, F32)
@@ -195,21 +181,24 @@
     def arrive(k, carry):
         peer = tile_peer(k)
         wave_copy(peer, peer).wait_recv()
-        bin_copy(peer, peer).wait_recv()
         return carry
 
     lax.fori_loop(1, tiles, arrive, 0)
 
     names = []
     for q in range(tiles // 4):
-        names.append(recvb[4 * q] + recvb[4 * q + 1] + recvb[4 * q + 2] + recvb[4 * q + 3])
+        both = recvw[4 * q, CAP:, :].astype(F32)
+        for t in range(4 * q + 1, 4 * q + 4):
+            both = both + recvw[t, CAP:, :].astype(F32)
+        names.append(32.0 * both[0:1, :] + both[1:2, :])
     names = jnp.concatenate(names, axis=1)
     block = 256
+    arrived = recvw[:, 0:CAP, :].reshape(tiles * CAP, steps)
     order = [0, pixels - block] + [s for s in range(block, pixels - block, block)]
     for start in order:
         wanted = (iota((block, tiles * CAP), 0) + start).astype(F32)
         onehot = (wanted == names).astype(F32).astype(BF16)
-        grid[span + start : span + start + block, :] = dot(onehot, recvw[...]).astype(BF16)
+        grid[span + start : span + start + block, :] = dot(onehot, arrived).astype(BF16)
 
     @pl.when(has_up)
     def _():
@@ -402,44 +391,58 @@
     tail = jnp.logical_and(iota(share.shape, 0) + chip * part >= small, core == 1)
     gathered[core, chip] = jnp.where(tail, rest, share).astype(BF16)
 
-    def spread_copy(device, source):
-        return pltpu.make_async_remote_copy(
-            src_ref=gathered.at[core, chip], dst_ref=gathered.at[core, source],
-            send_sem=n_send.at[source], recv_sem=n_recv.at[source], device_id=device, device_id_type=MESH,
-        )
-
-    def spread_start(k, carry):
-        q, device = group_peer(k)
-        pltpu.make_async_remote_copy(
-            src_ref=gathered.at[core, chip], dst_ref=gathered.at[core, chip],
-            send_sem=n_send.at[q], recv_sem=n_recv.at[chip], device_id=device, device_id_type=MESH,
-        ).start()
-        return carry
-
-    lax.fori_loop(1, groups, spread_start, 0)
-
-    def forward(q, which):
-        return pltpu.make_async_remote_copy(
-            src_ref=gathered.at[which, q], dst_ref=gathered.at[which, q],
-            send_sem=f_send.at[q], recv_sem=f_recv.at[q],
+    def line_copy(b, source):
+        spot = at_outer * inner + source
+        return pltpu.make_async_remote_copy(
+            src_ref=gathered.at[core, spot], dst_ref=gathered.at[core, spot],
+            send_sem=n_send.at[b], recv_sem=n_recv.at[source],
+            device_id=device_at(at_outer, b), device_id_type=MESH,
+        )
+
+    def plane_copy(a, source):
+        spots = pl.ds(source * inner, inner)
+        return pltpu.make_async_remote_copy(
+            src_ref=gathered.at[core, spots], dst_ref=gathered.at[core, spots],
+            send_sem=m_send.at[a], recv_sem=m_recv.at[source],
+            device_id=device_at(a, at_inner), device_id_type=MESH,
+        )
+
+    def forward(a, which):
+        spots = pl.ds(a * inner, inner)
+        return pltpu.make_async_remote_copy(
+            src_ref=gathered.at[which, spots], dst_ref=gathered.at[which, spots],
+            send_sem=f_send.at[a], recv_sem=f_recv.at[a],
             device_id={"tile": partner, "rep": rep}, device_id_type=MESH,
         )
 
-    forward(chip, core).start()
-
-    def pass_on(k, carry):
-        q, device = group_peer(groups - k)
-        spread_copy(device, q).wait_recv()
-        forward(q, core).start()
-        return carry
-
-    lax.fori_loop(1, groups, pass_on, 0)
-
-    def finish(q, carry):
-        forward(q, 1 - core).wait_recv()
-        return carry
-
-    lax.fori_loop(0, groups, finish, 0)
+    for b in range(inner):
+
+        @pl.when(at_inner != b)
+        def _():
+            line_copy(b, at_inner).start()
+
+    for b in range(inner):
+
+        @pl.when(at_inner != b)
+        def _():
+            line_copy(b, b).wait_recv()
+
+    for a in range(outer):
+
+        @pl.when(at_outer != a)
+        def _():
+            plane_copy(a, at_outer).start()
+
+    forward(at_outer, core).start()
+    for a in range(outer):
+
+        @pl.when(at_outer != a)
+        def _():
+            plane_copy(a, a).wait_recv()
+            forward(a, core).start()
+
+    for a in range(outer):
+        forward(a, 1 - core).wait_recv()
 
     out_ref[...] = gathered[...]
 
@@ -456,7 +459,6 @@
     def sent(k, carry):
         peer = tile_peer(k)
         wave_copy(peer, me).wait_send()
-        bin_copy(peer, me).wait_send()
         return carry
 
     lax.fori_loop(1, tiles, sent, 0)
@@ -474,18 +476,18 @@
             share_copy(b, at_inner).wait_send()
 
 
-    def shared(k, carry):
-        q, device = group_peer(k)
-        spread_copy(device, q).wait_send()
-        return carry
-
-    lax.fori_loop(1, groups, shared, 0)
-
-    def passed(q, carry):
-        forward(q, core).wait_send()
-        return carry
-
-    lax.fori_loop(0, groups, passed, 0)
+    for b in range(inner):
+
+        @pl.when(at_inner != b)
+        def _():
+            line_copy(b, at_inner).wait_send()
+
+    for a in range(outer):
+        forward(a, core).wait_send()
+
+        @pl.when(at_outer != a)
+        def _():
+            plane_copy(a, at_outer).wait_send()
 
 
 def finish_kernel(
@@ -558,10 +560,8 @@
             pltpu.VMEM((3, 3, channels), BF16),
             pltpu.SMEM((1,), F32),
             dma((8,)),
-            pltpu.VMEM((tiles * CAP, steps), BF16),
-            pltpu.VMEM((tiles, 1, 128), F32),
-            pltpu.VMEM((tiles * CAP, steps), BF16),
-            pltpu.VMEM((tiles, 1, 128), F32),
+            pltpu.VMEM((tiles, CAP + 8, steps), BF16),
+            pltpu.VMEM((tiles, CAP + 8, steps), BF16),
             pltpu.VMEM(((height + 2 * HALO) * width, steps), BF16),
             pltpu.VMEM(((height + 2 * HALO) * width, 3 * steps), BF16),
             pltpu.VMEM((pixels, channels), F32),
@@ -577,10 +577,10 @@
             pltpu.VMEM((outer, inner * part, channels), F32),
             pltpu.VMEM((inner, part, channels), F32),
             pltpu.VMEM((2, groups, part, channels), BF16),
-            dma((tiles,)), dma((tiles,)), dma((tiles,)), dma((tiles,)),
+            dma((tiles,)), dma((tiles,)),
             dma((2,)), dma((2,)), dma((2,)), dma((2,)),
             dma((outer,)), dma((outer,)), dma((outer,)), dma((outer,)), dma((inner,)), dma((inner,)),
-            dma((groups,)), dma((groups,)), dma((groups,)), dma((groups,)),
+            dma((inner,)), dma((inner,)), dma((outer,)), dma((outer,)), dma((outer,)), dma((outer,)),
         ],
         compiler_params=pltpu.CompilerParams(
             collective_id=0, has_side_effects=True, vmem_limit_bytes=60 * 1024 * 1024

time: 41.9 us -> 42.4 us (1.012)
  Pallas kernels: 40.4 us -> 40.9 us
    pallas_call x1, Pallas kernels: 38.1 us -> 38.6 us  [on_device(): pl.pallas_call(functools.partial(step_kernel, tiles, reps, part), out_sha...]
where the time goes in v4:
time: 42.4 us; the launch traced here: 42.2 us
  Pallas kernels  40.9 us (96%)
  between operations  1.29 us (3%)
    pallas_call x1, Pallas kernels, on_device(): pl.pallas_call(functools.partial(step_kernel, tiles, reps, part), out_sha...  38.6 us
    pallas_call x1, Pallas kernels, on_device(): pl.pallas_call(finish_kernel, out_shape=(jax.ShapeDtypeStruct((height, wi...  2.28 us

profile of v4, /device:TPU:1, one launch (start us, length us, event | category | flops | bytes accessed | tf_op | source)
XLA Modules:
  0.0 42.2 jit_solution(9008673015481893650)
XLA Ops:
  1.3 38.6 %step.1 = (f32[8,128]{1,0:T(8,128)}, bf16[2,16,40,128]{3,2,1,0:T(8,128)(2,1)}) custom-call(s32[1,512]{1,0:T(1,128)} %bitcast.10, s32[1,512]{1,0:T(1,128)} %bin_hbm.1, bf16[512,128]{1,0:T(8,128)(2,1)} %bitcast.8, f32[8,128]{1,0:T(8,128)} %bitcast.9, bf16[3,384,128]{2,1,0:T(8,128)(2,1)} %bitcast.7, f32[1,128]{1,0:T(1,128)} %bitcast.11, ...), custom_call_target="tpu_custom_call" | custom-call | tf_op jit(solution)/shard_map/step/pallas_call | solution.py:545
  39.9 2.3 %finish.1 = (f32[8,128]{1,0:T(8,128)}, f32[3,3,128,128]{3,2,1,0:T(8,128)}, f32[1,128]{1,0:T(1,128)}, f32[3,3,128]{2,1,0:T(4,128)}) custom-call(f32[8,128]{1,0:T(8,128)} %get-tuple-element.10.pred_ref, bf16[2,16,40,128]{3,2,1,0:T(8,128)(2,1)} %get-tuple-element.11.gathered), custom_call_target="tpu_custom_call" | custom-call | tf_op jit(solution)/shard_map/finish/pallas_call | solution.py:593
